TPU v7x, 32 devices: a whole 2x2x4 slice. The times are simulated.
32 devices in a mesh: dp: 8 (over z, x), state: 4 (over y, core).
Axes of the slice: x: 2, y: 2, z: 4, core: 2. Of those that a mesh axis runs over, the one named last changes fastest.
Arguments:
- block_input: bfloat16 [8192, 2048], P(('dp', 'state')), may hold values from -6 to 6
- width_index: int32 [8], P('dp'), may hold values from 0 to 3
- w_in: bfloat16 [2048, 8512], P('dp', 'state'), may hold values from -0.125 to 0.125
- w_out: bfloat16 [4096, 2048], P('state', 'dp'), may hold values from -0.1875 to 0.1875
- conv_weight: float32 [4, 4352], replicated, may hold values from -3 to 3
- conv_bias: float32 [4352], replicated, may hold values from -2 to 2
- dt_bias: float32 [64], replicated, may hold values from -7 to -3.5
- a_log: float32 [64], replicated, may hold values from 0 to 0.7
- d_skip: float32 [64], replicated, may hold values from 0.5 to 1.5
- norm_in_gain: float32 [2048], replicated, may hold values from 0.5 to 1.5
- norm_out_gain: float32 [4096], replicated, may hold values from 0.5 to 1.5
- out_cotangent: bfloat16 [8192, 2048], P(('dp', 'state')), may hold values from -6 to 6
Outputs:
- block_out: bfloat16 [8192, 2048], P(('dp', 'state'))
- grad_input: float32 [8192, 2048], P(('dp', 'state'))
- grad_in_proj: float32 [2048, 8512], P('dp', 'state')
- grad_out_proj: float32 [4096, 2048], P('state', 'dp')
- grad_conv_weight: float32 [4, 4352], replicated
- grad_conv_bias: float32 [4352], replicated
- grad_dt_bias: float32 [64], replicated
- grad_a_log: float32 [64], replicated
- grad_d_skip: float32 [64], replicated
- grad_norm_in: float32 [2048], replicated
- grad_norm_out: float32 [4096], replicated
Inputs may be any that keep to these rules, and one draw needn't show every extreme that they name: `width_index`: a sequence of level w uses the first 64 / 8 * 2^w heads.
All inputs are finite; a program needn't handle non-finite values.
Results may differ from a plain program's by a relative error of at most 0.015.
Values may be sent and summed in bfloat16 or wider, within the bound.
No kernel may reach another device: no remote copies, remote signals or barrier semaphores. Data moves between devices by JAX's collectives and lax.ppermute only.
A program may use at most 192 MiB of HBM per device.

v0:
```python
import functools

import jax
import jax.numpy as jnp
from jax import lax
from jax.experimental import pallas as pl
from jax.experimental.pallas import tpu as pltpu
from jax.sharding import PartitionSpec as P

H = 64
P_SIZE = 64
N = 128
SPAN = 256
CONV = 4
EPSILON = 1e-05
F32 = jnp.float32
BF16 = jnp.bfloat16


def flip(value, axis, bit):
    return lax.ppermute(value, axis, [(i, i ^ bit) for i in range(lax.axis_size(axis))])


def moves(count, from_range, to_range):
    found = {}
    for source in range(count):
        for target in range(count):
            a, b = from_range(source), to_range(target)
            if source != target and max(a[0], b[0]) < min(a[1], b[1]):
                found.setdefault(target - source, []).append((source, target))
    return found


def stack_rows(parts, places):
    rows, width = parts[0].shape

    def kernel(places_ref, *refs):
        out = refs[-1]
        for i, part in enumerate(refs[:-1]):
            out[pl.ds(pl.multiple_of(places_ref[i] * rows, rows), rows), :] = part[...]

    return pl.pallas_call(
        kernel,
        in_specs=[pl.BlockSpec(memory_space=pltpu.SMEM)]
        + [pl.BlockSpec(memory_space=pltpu.VMEM) for _ in parts],
        out_specs=pl.BlockSpec(memory_space=pltpu.VMEM),
        out_shape=jax.ShapeDtypeStruct((rows * len(parts), width), parts[0].dtype),
    )(places, *parts)


def gather_state(own):
    count, here = lax.axis_size("state"), lax.axis_index("state")
    held = {0: own}
    bit = count // 2
    while bit:
        for key in list(held):
            held[key | bit] = flip(held[key], "state", bit)
        bit //= 2
    keys = sorted(held)
    return stack_rows([held[key] for key in keys], here ^ jnp.array(keys))


def ringed(axis):
    return lax.axis_size(axis) <= 8


def to_ring(value, axis):
    if not ringed(axis):
        return value
    count, here = lax.axis_size(axis), lax.axis_index(axis)
    steps = count // 2
    pair = value.shape[1] // count
    sides = []
    for side in range(2):
        blocks = [value[:, (2 * i + side) * pair : (2 * i + side + 1) * pair] for i in range(steps)][::-1]
        turned = jnp.concatenate(blocks + blocks[:-1], axis=1)
        sides.append(lax.dynamic_slice_in_dim(turned, (steps - 1 - here // 2) * pair, steps * pair, 1))
    even = here % 2 == 0
    return jnp.concatenate([jnp.where(even, *sides), jnp.where(even, *sides[::-1])], axis=1)


def from_ring(value, axis):
    if not ringed(axis):
        return value
    count, here = lax.axis_size(axis), lax.axis_index(axis)
    steps = count // 2
    pair = value.shape[1] // count
    first, second = value[:, : steps * pair], value[:, steps * pair :]
    even = here % 2 == 0
    sides = []
    for side in (jnp.where(even, first, second), jnp.where(even, second, first)):
        blocks = [side[:, i * pair : (i + 1) * pair] for i in range(steps)][::-1]
        turned = jnp.concatenate(blocks + blocks[:-1], axis=1)
        sides.append(lax.dynamic_slice_in_dim(turned, (steps - 1 - here // 2) * pair, steps * pair, 1))
    return jnp.concatenate(
        [sides[i % 2][:, i // 2 * pair : (i // 2 + 1) * pair] for i in range(count)], axis=1
    )


def gather_dp(own):
    count = lax.axis_size("dp")
    if not ringed("dp"):
        return [lax.all_gather(own, "dp", axis=1, tiled=True)]
    ring = [(i, (i + 2) % count) for i in range(count)]
    mine, other = [own], []
    for step in range(count // 2):
        other.append(flip(mine[step], "dp", 1))
        if step + 1 < count // 2:
            mine.append(lax.ppermute(mine[step], "dp", ring))
    return mine + other


def scatter_dp(left, right):
    count = lax.axis_size("dp")

    def multiply(some, kind):
        return lax.dot_general(left, some, (((0,), (0,)), ((), ())), preferred_element_type=kind)

    if not ringed("dp"):
        return lax.psum_scatter(multiply(right, F32), "dp", scatter_dimension=1, tiled=True)
    steps = count // 2
    half = right.shape[1] // 2
    wide = half // steps
    ring = [(i, (i + 2) % count) for i in range(count)]
    other = multiply(right[:, half:], BF16)
    mine = multiply(right[:, :half], BF16)
    carried = None
    for step in range(1, steps + 1):
        at = step % steps * wide
        came = flip(other[:, at : at + wide], "dp", 1)
        total = mine[:, at : at + wide].astype(F32) + came.astype(F32)
        if carried is not None:
            total = total + carried.astype(F32)
        if step < steps:
            carried = lax.ppermute(total.astype(BF16), "dp", ring)
    return total


def scatter_state(whole):
    count, here = lax.axis_size("state"), lax.axis_index("state")
    rows = whole.reshape(count, whole.shape[0] // count, whole.shape[1])
    parts = {key: lax.dynamic_index_in_dim(rows, here ^ key, 0, keepdims=False) for key in range(count)}
    bit = 1
    while bit < count:
        for key in [k for k in parts if not k & bit]:
            sent = flip(parts.pop(key | bit).astype(BF16), "state", bit)
            parts[key] = parts[key].astype(F32) + sent.astype(F32)
        bit *= 2
    return parts[0]


def sum_axis(value, axis):
    bits = []
    while 1 << len(bits) < lax.axis_size(axis):
        bits.append(1 << len(bits))
    for bit in bits:
        value = value + flip(value, axis, bit)
    return value


def meet(first, second):
    low, high = max(first[0], second[0]), min(first[1], second[1])
    return (low, high) if low < high else None


def cut_rows(own, group, plans):
    groups = len(plans[0])
    store, width = own.shape
    sizes = [max(sum(b - a for a, b in ranges) for ranges in plan if ranges) for plan in plans]

    def kernel(group_ref, own_ref, *outs):
        for out in outs:
            out[...] = jnp.zeros_like(out)
        for g in range(groups):

            @pl.when(group_ref[0] == g)
            def _():
                for out, plan in zip(outs, plans):
                    at = 0
                    for ask in plan[g] or []:
                        found = meet(ask, (store * g, store * (g + 1)))
                        if found:
                            low, high = found
                            out[at + low - ask[0] : at + high - ask[0], :] = own_ref[low - store * g : high - store * g, :]
                        at += ask[1] - ask[0]

    return pl.pallas_call(
        kernel,
        in_specs=[pl.BlockSpec(memory_space=pltpu.SMEM), pl.BlockSpec(memory_space=pltpu.VMEM)],
        out_specs=[pl.BlockSpec(memory_space=pltpu.VMEM) for _ in plans],
        out_shape=[jax.ShapeDtypeStruct((size, width), BF16) for size in sizes],
        name="cut_rows",
    )(group[None], own)


def paste_rows(pieces, group, plans, store):
    groups = len(plans[0])
    width = pieces[0].shape[1]

    def kernel(group_ref, *refs):
        out = refs[-1]
        out[...] = jnp.zeros_like(out)
        for g in range(groups):

            @pl.when(group_ref[0] == g)
            def _():
                for piece, plan in zip(refs[:-1], plans):
                    at = 0
                    for ask in plan[g] or []:
                        found = meet(ask, (store * g, store * (g + 1)))
                        if found:
                            low, high = found
                            out[low - store * g : high - store * g, :] += piece[
                                at + low - ask[0] : at + high - ask[0], :
                            ].astype(F32)
                        at += ask[1] - ask[0]

    return pl.pallas_call(
        kernel,
        in_specs=[pl.BlockSpec(memory_space=pltpu.SMEM)]
        + [pl.BlockSpec(memory_space=pltpu.VMEM) for _ in pieces],
        out_specs=pl.BlockSpec(memory_space=pltpu.VMEM),
        out_shape=jax.ShapeDtypeStruct((store, width), F32),
        name="paste_rows",
    )(group[None], *pieces)


def spans(size):
    half = size // 2
    return [(0, half, half), (half, size, size)]


def dots(left, right, contract, exact=False):
    return lax.dot_general(
        left,
        right,
        (contract, ((), ())),
        preferred_element_type=F32,
        precision=lax.Precision.HIGHEST if exact else None,
    )


def softplus(value):
    return jnp.maximum(value, 0.0) + jnp.log1p(jnp.exp(-jnp.abs(value)))


def triangle(size, upper):
    row = lax.broadcasted_iota(jnp.int32, (size, size), 0)
    col = lax.broadcasted_iota(jnp.int32, (size, size), 1)
    return (row <= col if upper else row >= col).astype(F32)


def decays(raw, place, bias, bias_t, rate, rate_t):
    pre = dots(raw, place, ((1,), (1,))) + bias
    pre_t = dots(place, raw, ((1,), (1,))) + bias_t
    step, step_t = softplus(pre), softplus(pre_t)
    size = raw.shape[0]
    log = dots(triangle(size, False), step * rate, ((1,), (0,)), True)
    log_t = dots(step_t * rate_t, triangle(size, True), ((1,), (0,)), True)
    return pre, step, step_t, log, log_t


def decay_of(log, log_t, head, span):
    first, last, seen = span
    gap = log[first:last, head : head + 1] - log_t[head : head + 1, :seen]
    row = first + lax.broadcasted_iota(jnp.int32, gap.shape, 0)
    col = lax.broadcasted_iota(jnp.int32, gap.shape, 1)
    return jnp.exp(jnp.where(row >= col, gap, -jnp.inf))


def convolve(before, here, taps, bias):
    ext = jnp.concatenate([before, here], axis=0)
    size = here.shape[0]
    start = before.shape[0] - (CONV - 1)
    total = bias + taps[0:1] * ext[start : start + size]
    for offset in range(1, CONV):
        total = total + taps[offset : offset + 1] * ext[start + offset : start + offset + size]
    return total, ext


def join(pieces, whole):
    @pl.when(pl.program_id(0) == 0)
    def _():
        wide = pieces[0].shape[1]
        for i, piece in enumerate(pieces):
            whole[:, i * wide : (i + 1) * wide] = piece[...]


def joined(pieces):
    return pltpu.VMEM((pieces[0].shape[0], sum(p.shape[1] for p in pieces)), BF16)


def row_of_sums(value):
    total = value[:, :128]
    for at in range(128, value.shape[1], 128):
        total = total + value[:, at : at + 128]
    return dots(jnp.ones((8, 128), F32), total, ((1,), (1,)), True)


def scan_forward(is_first, *refs):
    x_ref, taps_ref, cbias_ref, place_ref, bias_ref, bias_t_ref, rate_ref, rate_t_ref, skip_ref = refs[:9]
    act_ref, mixed_ref, starts_ref, halo, state = refs[-5:]

    @pl.when(pl.program_id(0) == 0)
    def _():
        for new, old in zip((halo, state), refs[-7:-5]):
            new[...] = jnp.zeros_like(new) if is_first else old[...]

    size = x_ref.shape[0]
    heads = place_ref.shape[0]
    cols = heads * P_SIZE
    wide = cols + 2 * N
    for at in range(0, wide, 128):
        here = x_ref[:, at : at + 128].astype(F32)
        conv, _ = convolve(halo[:, at : at + 128], here, taps_ref[:, at : at + 128], cbias_ref[:, at : at + 128])
        act_ref[:, at : at + 128] = (conv * jax.nn.sigmoid(conv)).astype(BF16)
        halo[:, at : at + 128] = here[size - 8 :]
    _, step, step_t, log, log_t = decays(
        x_ref[:, wide:], place_ref[...], bias_ref[...], bias_t_ref[...], rate_ref[...], rate_t_ref[...]
    )
    growth = jnp.exp(log)
    tail = jnp.exp(log[size - 1 :] - log) * step
    inputs_b = act_ref[:, cols : cols + N]
    readout = act_ref[:, cols + N :]
    scores = dots(readout, inputs_b, ((1,), (1,)))
    left = lax.broadcasted_iota(jnp.int32, (size, 128), 1) < P_SIZE
    upper = lax.broadcasted_iota(jnp.int32, (128, 128), 0) < P_SIZE
    for pair in range(heads // 2):
        at = pair * 128
        a, b = 2 * pair, 2 * pair + 1
        vals = act_ref[:, at : at + 128]
        vals_f = vals.astype(F32)
        held = state[at : at + 128, :]
        starts_ref[at : at + 128, :] = held
        outer = dots(readout, held.astype(BF16), ((1,), (1,)))
        base = jnp.where(left, growth[:, a : a + 1], growth[:, b : b + 1]) * outer + skip_ref[:, at : at + 128] * vals_f
        split = [jnp.where(left, vals, 0), jnp.where(left, 0, vals)]
        for span in spans(size):
            first, last, seen = span
            total = base[first:last]
            for head, part in ((a, split[0]), (b, split[1])):
                mix = scores[first:last, :seen] * decay_of(log, log_t, head, span) * step_t[head : head + 1, :seen]
                total = total + dots(mix.astype(BF16), part[:seen], ((1,), (0,)))
            mixed_ref[first:last, at : at + 128] = total
        low = (vals_f * jnp.where(left, tail[:, a : a + 1], tail[:, b : b + 1])).astype(BF16)
        keep = jnp.where(upper, growth[size - 1 :, a : a + 1], growth[size - 1 :, b : b + 1])
        state[at : at + 128, :] = keep * held + dots(low, inputs_b, ((0,), (0,)))


def scan_backward(is_last, is_first, *refs):
    (
        x_ref, before_ref, act_ref, grad_ref, starts_ref,
        taps_ref, cbias_ref, place_ref, bias_ref, bias_t_ref, rate_ref, rate_t_ref, skip_ref,
    ) = refs[:13]
    olds = refs[13:-12]
    out_ref, *news = refs[-12:-6]
    by_col, by_row, tails, score_sum, in_grad, read_grad = refs[-6:]
    for i, new in enumerate(news):
        new[...] = jnp.zeros_like(new) if is_last else olds[i + 1][...]
    after, state, conv_ref, skip_grad_ref, head_ref = news
    size = x_ref.shape[0]
    heads = place_ref.shape[0]
    cols = heads * P_SIZE
    wide = cols + 2 * N
    place = place_ref[...]
    pre, step, step_t, log, log_t = decays(
        x_ref[:, wide:], place, bias_ref[...], bias_t_ref[...], rate_ref[...], rate_t_ref[...]
    )
    growth = jnp.exp(log)
    tail_exp = jnp.exp(log[size - 1 :] - log)
    tail = tail_exp * step
    inputs_b = act_ref[:, cols : cols + N]
    readout = act_ref[:, cols + N :]
    scores = dots(readout, inputs_b, ((1,), (1,)))
    left = lax.broadcasted_iota(jnp.int32, (size, 128), 1) < P_SIZE
    upper = lax.broadcasted_iota(jnp.int32, (128, 128), 0) < P_SIZE

    def through_conv(at, grad):
        here = x_ref[:, at : at + 128].astype(F32)
        before = before_ref[8:, at : at + 128].astype(F32)
        if is_first:
            before = jnp.zeros_like(before)
        taps = taps_ref[:, at : at + 128]
        conv, ext = convolve(before, here, taps, cbias_ref[:, at : at + 128])
        sig = jax.nn.sigmoid(conv)
        grad = grad * (sig * (1.0 + conv * (1.0 - sig)))
        start = 8 - (CONV - 1)
        rows = [jnp.sum(grad * ext[start + o : start + o + size], axis=0, keepdims=True) for o in range(CONV)]
        rows += [jnp.sum(grad, axis=0, keepdims=True), jnp.zeros((3, 128), F32)]
        conv_ref[:, at : at + 128] += jnp.concatenate(rows, axis=0)
        onward = jnp.concatenate([grad, after[:, at : at + 128]], axis=0)
        after[:, at : at + 128] = grad[:8]
        total = taps[CONV - 1 : CONV] * grad
        for o in range(CONV - 1):
            total = total + taps[o : o + 1] * onward[CONV - 1 - o : CONV - 1 - o + size]
        out_ref[:, at : at + 128] = total.astype(BF16)

    score_sum[...] = jnp.zeros_like(score_sum)
    in_grad[...] = jnp.zeros_like(in_grad)
    read_grad[...] = jnp.zeros_like(read_grad)
    for pair in range(heads // 2):
        at = pair * 128
        a, b = 2 * pair, 2 * pair + 1
        vals = act_ref[:, at : at + 128]
        vals_f = vals.astype(F32)
        grad = grad_ref[:, at : at + 128]
        grad_f = grad.astype(F32)
        starts = starts_ref[at : at + 128, :]
        starts_low = starts.astype(BF16)
        held = state[at : at + 128, :]
        held_low = held.astype(BF16)
        grown = grad_f * jnp.where(left, growth[:, a : a + 1], growth[:, b : b + 1])
        outer_low = grown.astype(BF16)
        outer = grown * dots(readout, starts_low, ((1,), (1,)))
        read_grad[...] += dots(outer_low, starts_low, ((1,), (0,)))
        tail_pair = jnp.where(left, tail[:, a : a + 1], tail[:, b : b + 1])
        low = (vals_f * tail_pair).astype(BF16)
        in_grad[...] += dots(low, held_low, ((1,), (0,)))
        low_grad = dots(inputs_b, held_low, ((1,), (1,)))
        tail_part = low_grad * vals_f
        product = grad_f * vals_f
        skip_grad_ref[:, at : at + 128] += jnp.sum(product, axis=0, keepdims=True)
        keep = jnp.where(upper, growth[size - 1 :, a : a + 1], growth[size - 1 :, b : b + 1])
        shared = jnp.sum(held * starts, axis=1, keepdims=True)
        state[at : at + 128, :] = dots(outer_low, readout, ((0,), (0,))) + keep * held
        base = skip_ref[:, at : at + 128] * grad_f + low_grad * tail_pair
        top = base[: size // 2]
        bottom = base[size // 2 :]
        for head, side in ((a, left), (b, jnp.logical_not(left))):
            own = jnp.where(side, grad, 0)
            tails[:, head : head + 1] = jnp.sum(jnp.where(side, tail_part, 0.0), axis=1, keepdims=True)
            rows = []
            sums = jnp.zeros((1, size), F32)
            for span in spans(size):
                first, last, seen = span
                mix_grad = dots(own[first:last], vals[:seen], ((1,), (1,)))
                decay = decay_of(log, log_t, head, span)
                steps = step_t[head : head + 1, :seen]
                some = scores[first:last, :seen]
                decayed = mix_grad * decay
                by_score = decayed * some
                score_sum[first:last, :seen] += decayed * steps
                rows.append(jnp.sum(by_score * steps, axis=1, keepdims=True))
                sums = sums + jnp.pad(jnp.sum(by_score, axis=0, keepdims=True), ((0, 0), (0, size - seen)))
                back = dots((some * decay * steps).astype(BF16), own[first:last], ((0,), (0,)))
                top = top + back[: size // 2]
                if seen == size:
                    bottom = bottom + back[size // 2 :]
            by_row[head : head + 1, :] = sums
            flow = jnp.sum(jnp.where(side, outer, 0.0), axis=1, keepdims=True)
            by_col[:, head : head + 1] = jnp.concatenate(rows, axis=0) + flow
            half = shared[:P_SIZE] if head == a else shared[P_SIZE:]
            by_col[size - 1 :, head : head + 1] += growth[size - 1 :, head : head + 1] * jnp.sum(
                half, axis=0, keepdims=True
            )
        through_conv(at, jnp.concatenate([top, bottom], axis=0))

    score_grad = score_sum[...].astype(BF16)
    through_conv(cols, in_grad[...] + dots(score_grad, readout, ((0,), (0,))))
    through_conv(cols + N, read_grad[...] + dots(score_grad, inputs_b, ((1,), (0,))))

    eye = (
        lax.broadcasted_iota(jnp.int32, (heads, heads), 0) == lax.broadcasted_iota(jnp.int32, (heads, heads), 1)
    ).astype(F32)
    summed = dots(by_row[...], eye, ((0,), (0,)), True)
    tail_grad = tails[...]
    tail_term = tail_grad * tail
    log_grad = by_col[...] - step * summed - tail_term
    row = lax.broadcasted_iota(jnp.int32, log_grad.shape, 0)
    log_grad = log_grad + jnp.where(row == size - 1, jnp.sum(tail_term, axis=0, keepdims=True), 0.0)
    decay_grad = dots(triangle(size, True), log_grad, ((1,), (0,)), True)
    step_grad = summed + tail_grad * tail_exp + decay_grad * rate_ref[...]
    raw = step_grad * jax.nn.sigmoid(pre)
    head_ref[...] += jnp.concatenate(
        [
            jnp.sum(raw, axis=0, keepdims=True),
            jnp.sum(decay_grad * step, axis=0, keepdims=True) * rate_ref[...],
            jnp.zeros((6, heads), F32),
        ],
        axis=0,
    )
    out_ref[:, wide:] = dots(raw.astype(BF16), place, ((1,), (0,))).astype(BF16)


def whole_spec(value):
    return pl.BlockSpec(value.shape, lambda k: (0,) * value.ndim)


def row_spec(value):
    return pl.BlockSpec((SPAN, value.shape[1]), lambda k: (k, 0))


def project_kernel(left_ref, *refs):
    *pieces, out_ref, whole = refs
    join(pieces, whole)
    out_ref[...] = dots(left_ref[...], whole[...], ((1,), (1,))).astype(BF16)


def run_project(left, pieces):
    out = jax.ShapeDtypeStruct((left.shape[0], pieces[0].shape[0]), BF16)
    return pl.pallas_call(
        project_kernel,
        grid=(left.shape[0] // TALL,),
        in_specs=[tall_spec(left)] + [whole_spec(p) for p in pieces],
        out_specs=tall_spec(out),
        out_shape=out,
        scratch_shapes=[joined(pieces)],
        compiler_params=pltpu.CompilerParams(dimension_semantics=("arbitrary",)),
        name="project",
    )(left, *pieces)


def run_scan_forward(x_proj, params):
    rows, width = x_proj.shape
    wide = params[0].shape[1]
    cols = wide - 2 * N
    blocks = rows // SPAN
    per = 2
    outs = [
        jax.ShapeDtypeStruct((rows, wide), BF16),
        jax.ShapeDtypeStruct((rows, cols), F32),
        jax.ShapeDtypeStruct((blocks * cols, N), F32),
    ]
    carried = [jax.ShapeDtypeStruct((8, wide), F32), jax.ShapeDtypeStruct((cols, N), F32)]
    held = None
    for at in range(0, blocks, per):
        args = [x_proj, *params]
        ins = [pl.BlockSpec((SPAN, width), lambda k, at=at: (at + k, 0))] + [whole_spec(p) for p in params]
        aliases = {}
        if held is not None:
            aliases = {len(args) + i: i for i in range(len(held))}
            ins += [pl.BlockSpec(memory_space=pl.ANY) for _ in outs] + [whole_spec(c) for c in carried]
            args += held
        held = pl.pallas_call(
            functools.partial(scan_forward, held is None),
            grid=(per,),
            in_specs=ins,
            out_specs=[
                pl.BlockSpec((SPAN, wide), lambda k, at=at: (at + k, 0)),
                pl.BlockSpec((SPAN, cols), lambda k, at=at: (at + k, 0)),
                pl.BlockSpec((cols, N), lambda k, at=at: (at + k, 0)),
            ]
            + [whole_spec(c) for c in carried],
            out_shape=outs + carried,
            input_output_aliases=aliases,
            compiler_params=pltpu.CompilerParams(dimension_semantics=("arbitrary",)),
        )(*args)
    return held[:3]


TALL = 2 * SPAN


def tall_spec(value):
    return pl.BlockSpec((TALL, value.shape[1]), lambda k: (k, 0))


def across_spec():
    return pl.BlockSpec((8, TALL), lambda k: (0, k))


def gate_kernel(*refs):
    normed_ref, mixed_ref, mask_ref, *pieces, gate_ref, square_ref, whole = refs
    join(pieces, whole)
    gate = dots(normed_ref[...], whole[...], ((1,), (1,))).astype(BF16)
    gate_ref[...] = gate
    gate = gate.astype(F32)
    gated = mixed_ref[...] * (gate * jax.nn.sigmoid(gate)) * mask_ref[...]
    square_ref[...] = row_of_sums(gated * gated)


def run_gate(normed, mixed, mask, pieces):
    rows, cols = mixed.shape
    return pl.pallas_call(
        gate_kernel,
        grid=(rows // TALL,),
        in_specs=[tall_spec(normed), tall_spec(mixed), whole_spec(mask)] + [whole_spec(p) for p in pieces],
        out_specs=[tall_spec(mixed), across_spec()],
        out_shape=[jax.ShapeDtypeStruct((rows, cols), BF16), jax.ShapeDtypeStruct((8, rows), F32)],
        scratch_shapes=[joined(pieces)],
        compiler_params=pltpu.CompilerParams(dimension_semantics=("arbitrary",)),
        name="gate_forward",
    )(normed, mixed, mask, *pieces)


def normalize_kernel(mixed_ref, gate_ref, scale_ref, gain_ref, out_ref):
    gate = gate_ref[...].astype(F32)
    gated = mixed_ref[...] * (gate * jax.nn.sigmoid(gate))
    out_ref[...] = (gated * scale_ref[...] * gain_ref[...]).astype(BF16)


def run_normalize(mixed, gate, scale, gain):
    return pl.pallas_call(
        normalize_kernel,
        grid=(mixed.shape[0] // SPAN,),
        in_specs=[row_spec(mixed), row_spec(gate), row_spec(scale), whole_spec(gain)],
        out_specs=row_spec(gate),
        out_shape=jax.ShapeDtypeStruct(gate.shape, BF16),
        name="normalize",
    )(mixed, gate, scale, gain)


def gate_grad_kernel(*refs):
    cot_ref, mixed_ref, gate_ref, scale_ref, gain_ref, mask_ref, *pieces, grad_ref, aligned_ref, norm_ref, whole = refs
    join(pieces, whole)
    grad = dots(cot_ref[...], whole[...], ((1,), (1,)))
    grad_ref[...] = grad
    gate = gate_ref[...].astype(F32)
    product = grad * (mixed_ref[...] * (gate * jax.nn.sigmoid(gate)) * mask_ref[...])
    aligned_ref[...] = row_of_sums(product * gain_ref[...])

    @pl.when(pl.program_id(0) == 0)
    def _():
        norm_ref[...] = jnp.zeros_like(norm_ref)

    norm_ref[...] += jnp.sum(product * scale_ref[...], axis=0, keepdims=True)


def run_gate_grad(cot, mixed, gate, scale, gain, mask, pieces):
    rows, cols = mixed.shape
    return pl.pallas_call(
        gate_grad_kernel,
        grid=(rows // TALL,),
        in_specs=[tall_spec(cot), tall_spec(mixed), tall_spec(gate), tall_spec(scale)]
        + [whole_spec(gain), whole_spec(mask)]
        + [whole_spec(p) for p in pieces],
        out_specs=[tall_spec(mixed), across_spec(), pl.BlockSpec((1, cols), lambda k: (0, 0))],
        out_shape=[
            jax.ShapeDtypeStruct((rows, cols), F32),
            jax.ShapeDtypeStruct((8, rows), F32),
            jax.ShapeDtypeStruct((1, cols), F32),
        ],
        scratch_shapes=[joined(pieces)],
        compiler_params=pltpu.CompilerParams(dimension_semantics=("arbitrary",)),
        name="gate_backward",
    )(cot, mixed, gate, scale, gain, mask, *pieces)


def run_products(lefts, piece_lists, against=None):
    rows = lefts[0].shape[0]
    count = len(lefts)
    number = len(piece_lists[0])
    wide = piece_lists[0][0].shape[1]
    flat = [piece for pieces in piece_lists for piece in pieces]
    others = [] if against is None else [against]

    def kernel(*refs):
        wholes = refs[-count:]
        other = refs[count + len(flat) : -count]
        total = None
        for at in range(count):
            join(refs[count + at * number : count + (at + 1) * number], wholes[at])
            part = dots(refs[at][...], wholes[at][...], ((1,), (0,)))
            total = part if total is None else total + part
        other[len(others)][...] = total.astype(BF16)
        if others:
            sums = jnp.sum(total * other[0][...].astype(F32), axis=0, keepdims=True)

            @pl.when(pl.program_id(0) == 0)
            def _():
                other[2][...] = sums

            @pl.when(pl.program_id(0) > 0)
            def _():
                other[2][...] += sums

    out = jax.ShapeDtypeStruct((rows, wide * number), BF16)
    sums = [jax.ShapeDtypeStruct((1, wide * number), F32)] * len(others)
    return pl.pallas_call(
        kernel,
        grid=(rows // TALL,),
        in_specs=[tall_spec(left) for left in lefts] + [whole_spec(p) for p in flat] + [tall_spec(o) for o in others],
        out_specs=[tall_spec(out)] + [whole_spec(total) for total in sums],
        out_shape=[out] + sums,
        scratch_shapes=[joined(pieces) for pieces in piece_lists],
        compiler_params=pltpu.CompilerParams(dimension_semantics=("arbitrary",)),
    )(*lefts, *flat, *others)


def run_scan_backward(x_proj, act, mixed_low, starts, params):
    rows, width = x_proj.shape
    wide = act.shape[1]
    cols = wide - 2 * N
    heads = cols // P_SIZE
    blocks = rows // SPAN
    carried = [
        jax.ShapeDtypeStruct((8, wide), F32),
        jax.ShapeDtypeStruct((cols, N), F32),
        jax.ShapeDtypeStruct((8, wide), F32),
        jax.ShapeDtypeStruct((1, cols), F32),
        jax.ShapeDtypeStruct((8, heads), F32),
    ]
    held = None
    for at in range(blocks - 1, -1, -1):
        ins = [
            pl.BlockSpec((SPAN, width), lambda k, at=at: (at, 0)),
            pl.BlockSpec((16, width), lambda k, at=at: (max(at * (SPAN // 16) - 1, 0), 0)),
            pl.BlockSpec((SPAN, wide), lambda k, at=at: (at, 0)),
            pl.BlockSpec((SPAN, cols), lambda k, at=at: (at, 0)),
            pl.BlockSpec((cols, N), lambda k, at=at: (at, 0)),
        ] + [whole_spec(p) for p in params]
        args = [x_proj, x_proj, act, mixed_low, starts, *params]
        aliases = {}
        if held is not None:
            aliases = {len(args) + i: i for i in range(len(held))}
            ins += [pl.BlockSpec(memory_space=pl.ANY)] + [whole_spec(c) for c in carried]
            args += held
        held = pl.pallas_call(
            functools.partial(scan_backward, held is None, at == 0),
            grid=(1,),
            in_specs=ins,
            out_specs=[pl.BlockSpec((SPAN, width), lambda k, at=at: (at, 0))] + [whole_spec(c) for c in carried],
            out_shape=[jax.ShapeDtypeStruct((rows, width), BF16)] + carried,
            input_output_aliases=aliases,
            scratch_shapes=[
                pltpu.VMEM((SPAN, heads), F32),
                pltpu.VMEM((heads, SPAN), F32),
                pltpu.VMEM((SPAN, heads), F32),
                pltpu.VMEM((SPAN, SPAN), F32),
                pltpu.VMEM((SPAN, N), F32),
                pltpu.VMEM((SPAN, N), F32),
            ],
        )(*args)
    return held[0], *held[3:]


def local(
    block_input,
    width_index,
    w_in,
    w_out,
    conv_weight,
    conv_bias,
    dt_bias,
    a_log,
    d_skip,
    norm_in_gain,
    norm_out_gain,
    out_cotangent,
):
    tok_rows, _ = block_input.shape
    inner = H * P_SIZE
    xbc = inner + 2 * N
    full_cols = 2 * inner + 2 * N + H
    groups, group = lax.axis_size("state"), lax.axis_index("state")
    seq_rows = tok_rows * groups
    heads = H // groups
    cols = inner // groups
    store = full_cols // groups

    def store_range(i):
        return (store * i, store * (i + 1))

    def value_range(i):
        return (inner + cols * i, inner + cols * (i + 1))

    def gate_range(i):
        return (cols * i, cols * (i + 1))

    def tail_range(i):
        return (inner + inner, full_cols)

    value_moves = moves(groups, store_range, value_range)
    tail_moves = moves(groups, store_range, tail_range)
    gate_moves = moves(groups, store_range, gate_range)

    def x_ranges(i):
        return [value_range(i), tail_range(i)]

    def at_shift(ranges, shift):
        return [ranges(g + shift) if 0 <= g + shift < groups else None for g in range(groups)]

    kinds = (("v", value_range, value_moves), ("b", tail_range, tail_moves), ("g", gate_range, gate_moves))
    sends = [(f"{kind}{abs(shift)}", ranges, shift, found[shift]) for kind, ranges, found in kinds for shift in sorted(found)]
    plans = [at_shift(x_ranges, 0), at_shift(lambda i: [gate_range(i)], 0)]
    plans += [at_shift(lambda i, ranges=ranges: [ranges(i)], shift) for _, ranges, shift, _ in sends]
    w_x_own, w_g_own, *cuts = cut_rows(w_in.T, group, plans)
    came = {"v": None, "b": None, "g": None}
    for (name, _, _, found), cut in zip(sends, cuts):
        part = lax.ppermute(cut, "state", found)
        came[name[0]] = part if came[name[0]] is None else came[name[0]] + part
    w_x_own = w_x_own + jnp.concatenate([came["v"], came["b"]], axis=0)
    w_g_own = w_g_own + came["g"]

    tokens = block_input.astype(F32)
    in_scale = lax.rsqrt(jnp.mean(tokens * tokens, axis=-1, keepdims=True) + EPSILON)
    normed = (tokens * in_scale * norm_in_gain).astype(BF16)

    w_x = gather_dp(w_x_own)
    normed_all = gather_state(to_ring(normed, "dp"))
    w_g = gather_dp(w_g_own)
    cot_all = gather_state(to_ring(out_cotangent, "dp"))
    w_o = gather_dp(w_out)

    own_heads = heads * group

    def own(entries, at, size):
        return lax.dynamic_slice_in_dim(entries, at, size, entries.ndim - 1)

    taps = jnp.concatenate([own(conv_weight, cols * group, cols), conv_weight[:, inner:]], axis=1)
    bias = jnp.concatenate([own(conv_bias, cols * group, cols), conv_bias[inner:]], axis=0)[None]
    gain_own = own(norm_out_gain, cols * group, cols)
    dt_own = own(dt_bias, own_heads, heads)
    rate_own = -jnp.exp(own(a_log, own_heads, heads))
    skip_own = jnp.repeat(own(d_skip, own_heads, heads), P_SIZE)[None]
    place = (own_heads + jnp.arange(heads)[:, None] == jnp.arange(H)[None, :]).astype(BF16)
    scan_params = (taps, bias, place, dt_own[None], dt_own[:, None], rate_own[None], rate_own[:, None], skip_own)
    x_proj = run_project(normed_all, w_x)
    act, mixed, starts = run_scan_forward(x_proj, scan_params)

    heads_on = H // 8 * jnp.left_shift(1, width_index[0])
    mask = ((cols * group + jnp.arange(cols)) // P_SIZE < heads_on).astype(F32)[None]
    active = (heads_on * P_SIZE).astype(F32)
    gain_mask = gain_own[None] * mask
    gate, square = run_gate(normed_all, mixed, mask, w_g)
    square = lax.psum(square[:1], "state")
    scale_row = lax.rsqrt(square / active + EPSILON)
    out_scale = scale_row.reshape(seq_rows, 1)
    normed_out = run_normalize(mixed, gate, out_scale, gain_mask)
    grad_out_proj = scatter_dp(normed_out, cot_all)

    out_grad, aligned, norm_sums = run_gate_grad(cot_all, mixed, gate, out_scale, gain_mask, mask, w_o)
    grad_norm_out = norm_sums[0]
    mixed, gate, out_grad = lax.optimization_barrier((mixed, gate, out_grad))
    gate_f = gate.astype(F32)
    gate_sig = jax.nn.sigmoid(gate_f)
    gate_act = gate_f * gate_sig
    gated = mixed * gate_act
    aligned = lax.psum(aligned[:1], "state").reshape(seq_rows, 1)
    pull = (aligned / active) * out_scale * out_scale * out_scale
    gated_grad = out_grad * gain_mask * out_scale - gated * mask * pull
    mixed_grad = gated_grad * gate_act
    gate_grad = (gated_grad * mixed * (gate_sig * (1.0 + gate_f * (1.0 - gate_sig)))).astype(BF16)

    (out_whole,) = run_products([normed_out], [w_o])
    block_out = (tokens + from_ring(scatter_state(out_whole), "dp")).astype(BF16)
    grad_in_gate = scatter_dp(gate_grad, normed_all)
    x_grad, conv_sums, skip_sums, head_sums = run_scan_backward(
        x_proj, act, mixed_grad.astype(BF16), starts, scan_params
    )
    taps_cols, bias_cols = conv_sums[:CONV], conv_sums[CONV]
    grad_d_skip = jnp.sum(skip_sums.reshape(heads, P_SIZE), axis=1)
    grad_dt_bias, grad_a_log = head_sums[0], head_sums[1]

    grad_in_x = scatter_dp(x_grad, normed_all)
    x_low, gate_low = grad_in_x.astype(BF16), grad_in_gate.astype(BF16)
    held = {"v": x_low[:cols], "b": x_low[cols:], "g": gate_low}
    pieces = [grad_in_x, grad_in_gate]
    plans = [at_shift(x_ranges, 0), at_shift(lambda i: [gate_range(i)], 0)]
    for name, ranges, shift, found in sends:
        pieces.append(lax.ppermute(held[name[0]], "state", [(b, a) for a, b in found]))
        plans.append(at_shift(lambda i, ranges=ranges: [ranges(i)], shift))
    grad_in_proj = paste_rows(pieces, group, plans, store).T

    normed_whole, gain_sums = run_products([x_grad, gate_grad], [w_x, w_g], normed_all)
    normed_grad = from_ring(scatter_state(normed_whole), "dp")
    pushed = normed_grad * norm_in_gain
    token_grad = in_scale * pushed - tokens * (
        in_scale * in_scale * in_scale * jnp.mean(pushed * tokens, axis=-1, keepdims=True)
    )
    grad_input = out_cotangent.astype(F32) + token_grad
    grad_norm_in = from_ring(gain_sums, "dp")[0] / norm_in_gain

    def spread(entries, total, at):
        return lax.dynamic_update_slice_in_dim(
            jnp.zeros(entries.shape[:-1] + (total,), F32), entries, at, entries.ndim - 1
        )

    taps_wide = spread(taps_cols[:, :cols], xbc, cols * group).at[:, inner:].set(taps_cols[:, cols:])
    bias_wide = spread(bias_cols[:cols], xbc, cols * group).at[inner:].set(bias_cols[cols:])
    flat = [
        taps_wide.reshape(-1),
        bias_wide,
        spread(grad_dt_bias, H, own_heads),
        spread(grad_a_log, H, own_heads),
        spread(grad_d_skip, H, own_heads),
        grad_norm_in,
        spread(grad_norm_out, inner, cols * group),
    ]
    sizes = [entry.shape[0] for entry in flat]
    packed = jnp.concatenate(flat)
    packed = jnp.pad(packed, (0, -packed.shape[0] % 1024)).reshape(-1, 128)
    packed = sum_axis(sum_axis(packed, "state"), "dp").reshape(-1)
    summed = []
    at = 0
    for size in sizes:
        summed.append(packed[at : at + size])
        at += size
    return (
        block_out,
        grad_input,
        grad_in_proj,
        grad_out_proj,
        summed[0].reshape(CONV, xbc),
        summed[1],
        summed[2],
        summed[3],
        summed[4],
        summed[5],
        summed[6],
    )


def solution(mesh):
    rows = P(("dp", "state"), None)
    whole = P()
    in_specs = (rows, P("dp"), P("dp", "state"), P("state", "dp")) + (whole,) * 7 + (rows,)
    out_specs = (rows, rows, P("dp", "state"), P("state", "dp")) + (whole,) * 7

    return jax.shard_map(local, mesh=mesh, in_specs=in_specs, out_specs=out_specs, check_vma=False)
```

profile of v0, /device:TPU:0, one launch (start us, length us, event | category | flops | bytes accessed | tf_op | source)
XLA Modules:
  0.0 601.2 jit_solution(15790188912425315710)
XLA Ops:
  38.5 9.6 %collective-permute-done.24.refs_2_.refs_7_ = bf16[1024,256]{1,0:T(8,128)(2,1)} collective-permute-done((bf16[1024,256]{1,0:T(8,128)(2,1)}, bf16[1024,256]{1,0:T(8,128)(2,1)}, u32[]{:S(2)}, u32[]{:S(2)}) %collective-permute-start.24) | collective-permute-done | bytes 524320 | tf_op jit(solution)/shard_map/ppermute | solution.py:109
  51.6 13.3 %collective-permute-done.16 = bf16[1024,256]{1,0:T(8,128)(2,1)S(1)} collective-permute-done((bf16[1024,256]{1,0:T(8,128)(2,1)S(1)}, bf16[1024,256]{1,0:T(8,128)(2,1)S(1)}, u32[]{:S(2)}, u32[]{:S(2)}) %collective-permute-start.16) | collective-permute-done | bytes 524320 | tf_op jit(solution)/shard_map/ppermute | solution.py:780
  81.4 9.9 %collective-permute-done.9.refs_2_.refs_4_ = bf16[1344,256]{1,0:T(8,128)(2,1)} collective-permute-done((bf16[1344,256]{1,0:T(8,128)(2,1)S(1)}, bf16[1344,256]{1,0:T(8,128)(2,1)}, u32[]{:S(2)}, u32[]{:S(2)}) %collective-permute-start.9) | collective-permute-done | bytes 688160 | tf_op jit(solution)/shard_map/ppermute | solution.py:109
  91.3 11.1 %collective-permute-done.17.refs_4_.refs_11_ = bf16[1024,256]{1,0:T(8,128)(2,1)S(1)} collective-permute-done((bf16[1024,256]{1,0:T(8,128)(2,1)S(1)}, bf16[1024,256]{1,0:T(8,128)(2,1)S(1)}, u32[]{:S(2)}, u32[]{:S(2)}) %collective-permute-start.17) | collective-permute-done | bytes 524320 | tf_op jit(solution)/shard_map/ppermute | solution.py:109
  108.8 19.7 %collective-permute-done.18.refs_5_.refs_12_ = bf16[1024,256]{1,0:T(8,128)(2,1)} collective-permute-done((bf16[1024,256]{1,0:T(8,128)(2,1)S(1)}, bf16[1024,256]{1,0:T(8,128)(2,1)}, u32[]{:S(2)}, u32[]{:S(2)}) %collective-permute-start.18) | collective-permute-done | bytes 524320 | tf_op jit(solution)/shard_map/ppermute | solution.py:109
  140.6 12.1 %collective-permute-done.19.refs_6_.refs_13_ = bf16[1024,256]{1,0:T(8,128)(2,1)S(1)} collective-permute-done((bf16[1024,256]{1,0:T(8,128)(2,1)}, bf16[1024,256]{1,0:T(8,128)(2,1)S(1)}, u32[]{:S(2)}, u32[]{:S(2)}) %collective-permute-start.19) | collective-permute-done | bytes 524320 | tf_op jit(solution)/shard_map/ppermute | solution.py:109
  173.9 12.0 %project.1.refs_0_.refs_1_ = bf16[1024,1344]{1,0:T(8,128)(2,1)} custom-call(bf16[1024,2048]{1,0:T(8,128)(2,1)} %shard_map.221.left_ref.refs_0_.refs_18_, bf16[1344,256]{1,0:T(8,128)(2,1)} %copy-done.12, bf16[1344,256]{1,0:T(8,128)(2,1)} %copy-done.18, bf16[1344,256]{1,0:T(8,128)(2,1)} %collective-permute-done.9.refs_2_.refs_4_, ...), custom_call_target="tpu_custom_call" | custom-call | tf_op jit(solution)/shard_map/project/pallas_call | solution.py:501
  185.8 10.8 %shard_map.222 = (bf16[1024,1280]{1,0:T(8,128)(2,1)}, f32[1024,1024]{1,0:T(8,128)}, f32[4096,128]{1,0:T(8,128)}, f32[8,1280]{1,0:T(8,128)}, f32[1024,128]{1,0:T(8,128)}) custom-call(bf16[1024,1344]{1,0:T(8,128)(2,1)} %project.1.refs_0_.refs_1_, f32[4,1280]{1,0:T(4,128)} %pad_maximum_fusion.2.refs_1_.refs_5_, f32[1,1280]{1,0:T(1,128)} %broadcast_in_dim.40.refs_2_.refs_6_, ...), custom_call_target="tpu_custom_call" | custom-call | tf_op jit(solution)/shard_map/pallas_call | solution.py:534
  196.6 11.0 %shard_map.223 = (bf16[1024,1280]{1,0:T(8,128)(2,1)}, f32[1024,1024]{1,0:T(8,128)}, f32[4096,128]{1,0:T(8,128)}, f32[8,1280]{1,0:T(8,128)}, f32[1024,128]{1,0:T(8,128)}) custom-call(bf16[1024,1344]{1,0:T(8,128)(2,1)} %project.1.refs_0_.refs_1_, ...), custom_call_target="tpu_custom_call", output_to_operand_aliasing={{0}: (9, {}), {1}: (10, {}), {2}: (11, {}), {3}: (12, {}), ... | custom-call | tf_op jit(solution)/shard_map/pallas_call | solution.py:534
  211.8 11.0 %gate_forward.1 = (bf16[1024,1024]{1,0:T(8,128)(2,1)}, f32[8,1024]{1,0:T(8,128)}) custom-call(bf16[1024,2048]{1,0:T(8,128)(2,1)} %shard_map.221.left_ref.refs_0_.refs_18_, f32[1024,1024]{1,0:T(8,128)} %get-tuple-element.104.refs_1_.mixed_ref, f32[1,1024]{1,0:T(1,128)} %compare_convert_fusion.refs_2_.refs_5_, bf16[1024,256]{1,0:T(8,128)(2,1)} %copy-done.13, ...), custom_call_target="tpu_custom_call" | custom-call | tf_op jit(solution)/shard_map/gate_forward/pallas_call | solution.py:574
  246.0 10.0 %collective-permute-done.30.refs_8_.refs_13_ = bf16[1024,256]{1,0:T(8,128)(2,1)} collective-permute-done((bf16[1024,256]{1,0:T(8,128)(2,1)}, bf16[1024,256]{1,0:T(8,128)(2,1)}, u32[]{:S(2)}, u32[]{:S(2)}) %collective-permute-start.30) | collective-permute-done | bytes 524320 | tf_op jit(solution)/shard_map/ppermute | solution.py:21
  256.0 12.6 %gate_backward.1 = (f32[1024,1024]{1,0:T(8,128)}, f32[8,1024]{1,0:T(8,128)}, f32[1,1024]{1,0:T(1,128)}) custom-call(bf16[1024,2048]{1,0:T(8,128)(2,1)} %shard_map.225.refs_0_, f32[1024,1024]{1,0:T(8,128)} %get-tuple-element.104.refs_1_.mixed_ref, bf16[1024,1024]{1,0:T(8,128)(2,1)} %get-tuple-element.105.gate_ref.refs_2_, f32[1024,1]{1,0:T(8,128)} %copy.64.scale_ref.refs_3_, ...), custom_call_target="tpu_custom_call" | custom-call | tf_op jit(solution)/shard_map/gate_backward/pallas_call | solution.py:621
  282.1 16.2 %shard_map.226 = (bf16[1024,1344]{1,0:T(8,128)(2,1)}, f32[8,1280]{1,0:T(8,128)}, f32[1024,128]{1,0:T(8,128)}, f32[8,1280]{1,0:T(8,128)}, f32[1,1024]{1,0:T(1,128)}, /*index=5*/f32[8,16]{1,0:T(8,128)}) custom-call(bf16[1024,1344]{1,0:T(8,128)(2,1)} %project.1.refs_0_.refs_1_, bf16[1024,1344]{1,0:T(8,128)(2,1)} %project.1.refs_0_.refs_1_, ...), custom_call_target="tpu_custom_call" | custom-call | tf_op jit(solution)/shard_map/pallas_call | solution.py:708
  298.3 16.6 %shard_map.227 = (bf16[1024,1344]{1,0:T(8,128)(2,1)}, f32[8,1280]{1,0:T(8,128)}, f32[1024,128]{1,0:T(8,128)}, f32[8,1280]{1,0:T(8,128)}, f32[1,1024]{1,0:T(1,128)}, /*index=5*/f32[8,16]{1,0:T(8,128)}) custom-call(bf16[1024,1344]{1,0:T(8,128)(2,1)} %project.1.refs_0_.refs_1_, ...), custom_call_target="tpu_custom_call", output_to_operand_aliasing={{0}: (13, {}), {1}: (14, {}), {2}: (15, {}), {3}: (16, {}),... | custom-call | tf_op jit(solution)/shard_map/pallas_call | solution.py:708
  314.9 16.8 %shard_map.228 = (bf16[1024,1344]{1,0:T(8,128)(2,1)}, f32[8,1280]{1,0:T(8,128)}, f32[1024,128]{1,0:T(8,128)}, f32[8,1280]{1,0:T(8,128)}, f32[1,1024]{1,0:T(1,128)}, /*index=5*/f32[8,16]{1,0:T(8,128)}) custom-call(bf16[1024,1344]{1,0:T(8,128)(2,1)} %project.1.refs_0_.refs_1_, ...), custom_call_target="tpu_custom_call", output_to_operand_aliasing={{0}: (13, {}), {1}: (14, {}), {2}: (15, {}), {3}: (16, {}),... | custom-call | tf_op jit(solution)/shard_map/pallas_call | solution.py:708
  331.7 16.5 %shard_map.229 = (bf16[1024,1344]{1,0:T(8,128)(2,1)}, f32[8,1280]{1,0:T(8,128)}, f32[1024,128]{1,0:T(8,128)}, f32[8,1280]{1,0:T(8,128)}, f32[1,1024]{1,0:T(1,128)}, /*index=5*/f32[8,16]{1,0:T(8,128)}) custom-call(bf16[1024,1344]{1,0:T(8,128)(2,1)} %project.1.refs_0_.refs_1_, ...), custom_call_target="tpu_custom_call", output_to_operand_aliasing={{0}: (13, {}), {1}: (14, {}), {2}: (15, {}), {3}: (16, {}),... | custom-call | tf_op jit(solution)/shard_map/pallas_call | solution.py:708
  373.5 20.3 %shard_map.230 = (bf16[1024,2048]{1,0:T(8,128)(2,1)}, f32[1,2048]{1,0:T(1,128)}) custom-call(bf16[1024,1344]{1,0:T(8,128)(2,1)} %get-tuple-element.126.refs_0_, bf16[1024,1024]{1,0:T(8,128)(2,1)} %get-tuple-element.137.refs_1_, bf16[1344,256]{1,0:T(8,128)(2,1)} %copy-done.12, bf16[1344,256]{1,0:T(8,128)(2,1)} %copy-done.18, ...), custom_call_target="tpu_custom_call" | custom-call | tf_op jit(solution)/shard_map/pallas_call | solution.py:669
  405.0 9.1 %shard_map.224 = bf16[1024,2048]{1,0:T(8,128)(2,1)} custom-call(bf16[1024,1024]{1,0:T(8,128)(2,1)} %normalize.1.refs_0_, bf16[1024,256]{1,0:T(8,128)(2,1)} %refs_6_.1, bf16[1024,256]{1,0:T(8,128)(2,1)} %collective-permute-done.24.refs_2_.refs_7_, bf16[1024,256]{1,0:T(8,128)(2,1)} %collective-permute-done.25.refs_3_.refs_8_, ...), custom_call_target="tpu_custom_call" | custom-call | tf_op jit(solution)/shard_map/pallas_call | solution.py:669
  467.0 17.5 %collective-permute-done.42 = bf16[1344,256]{1,0:T(8,128)(2,1)S(1)} collective-permute-done((bf16[1344,256]{1,0:T(8,128)(2,1)}, bf16[1344,256]{1,0:T(8,128)(2,1)S(1)}, u32[]{:S(2)}, u32[]{:S(2)}) %collective-permute-start.42) | collective-permute-done | bytes 688160 | tf_op jit(solution)/shard_map/ppermute | solution.py:21
  492.4 10.0 %collective-permute-done.66 = bf16[1024,256]{1,0:T(8,128)(2,1)S(1)} collective-permute-done((bf16[1024,256]{1,0:T(8,128)(2,1)S(1)}, bf16[1024,256]{1,0:T(8,128)(2,1)S(1)}, u32[]{:S(2)}, u32[]{:S(2)}) %collective-permute-start.66) | collective-permute-done | bytes 524320 | tf_op jit(solution)/shard_map/ppermute | solution.py:135
  504.8 8.9 %collective-permute-done.52 = bf16[1024,256]{1,0:T(8,128)(2,1)S(1)} collective-permute-done((bf16[1024,256]{1,0:T(8,128)(2,1)S(1)}, bf16[1024,256]{1,0:T(8,128)(2,1)S(1)}, u32[]{:S(2)}, u32[]{:S(2)}) %collective-permute-start.52) | collective-permute-done | bytes 524320 | tf_op jit(solution)/shard_map/ppermute | solution.py:135
  517.6 10.8 %collective-permute-done.45 = bf16[1344,256]{1,0:T(8,128)(2,1)S(1)} collective-permute-done((bf16[1344,256]{1,0:T(8,128)(2,1)S(1)}, bf16[1344,256]{1,0:T(8,128)(2,1)S(1)}, u32[]{:S(2)}, u32[]{:S(2)}) %collective-permute-start.45) | collective-permute-done | bytes 688160 | tf_op jit(solution)/shard_map/ppermute | solution.py:135
  528.7 10.9 %collective-permute-done.67 = bf16[1024,256]{1,0:T(8,128)(2,1)S(1)} collective-permute-done((bf16[1024,256]{1,0:T(8,128)(2,1)S(1)}, bf16[1024,256]{1,0:T(8,128)(2,1)S(1)}, u32[]{:S(2)}, u32[]{:S(2)}) %collective-permute-start.67) | collective-permute-done | bytes 524320 | tf_op jit(solution)/shard_map/ppermute | solution.py:135
  553.8 20.7 %collective-permute-done.39 = bf16[256,2048]{1,0:T(8,128)(2,1)S(1)} collective-permute-done((bf16[256,2048]{1,0:T(8,128)(2,1)S(1)}, bf16[256,2048]{1,0:T(8,128)(2,1)S(1)}, u32[]{:S(2)}, u32[]{:S(2)}) %collective-permute-start.39) | collective-permute-done | bytes 1048608 | tf_op jit(solution)/shard_map/ppermute | solution.py:21
  (454 shorter events, 280.6 us)
Async XLA Ops:
  26.8 53.4 %collective-permute-start.1 = (bf16[256,2048]{1,0:T(8,128)(2,1)S(1)}, bf16[256,2048]{1,0:T(8,128)(2,1)}, u32[]{:S(2)}, u32[]{:S(2)}) collective-permute-start(bf16[256,2048]{1,0:T(8,128)(2,1)S(1)} %pad_maximum_fusion.refs_0_), channel_id=1, source_target_pairs={{0,2},{1,3},{2,0},{3,1},{4,6},{5,7},{6,4},{7,5},{8,10},{9,11},{10,... | collective-permute-start | bytes 3145736 | tf_op jit(solution)/shard_map/ppermute | solution.py:21
  30.1 50.1 %collective-permute-start = (bf16[256,2048]{1,0:T(8,128)(2,1)S(1)}, bf16[256,2048]{1,0:T(8,128)(2,1)S(1)}, u32[]{:S(2)}, u32[]{:S(2)}) collective-permute-start(bf16[256,2048]{1,0:T(8,128)(2,1)S(1)} %pad_maximum_fusion.refs_0_), channel_id=1, source_target_pairs={{0,1},{1,0},{2,3},{3,2},{4,5},{5,4},{6,7},{7,6},{8,9},{9,8},{10,11... | collective-permute-start | bytes 3145736 | tf_op jit(solution)/shard_map/ppermute | solution.py:21
  64.9 37.6 %collective-permute-start.35 = (bf16[256,2048]{1,0:T(8,128)(2,1)S(1)}, bf16[256,2048]{1,0:T(8,128)(2,1)}, u32[]{:S(2)}, u32[]{:S(2)}) collective-permute-start(bf16[256,2048]{1,0:T(8,128)(2,1)S(1)} %pad_maximum_fusion.1.refs_0_), channel_id=1, source_target_pairs={{0,2},{1,3},{2,0},{3,1},{4,6},{5,7},{6,4},{7,5},{8,10},{9,11},{10,... | collective-permute-start | bytes 3145736 | tf_op jit(solution)/shard_map/ppermute | solution.py:21
  91.3 38.7 %collective-permute-start.10 = (bf16[1344,256]{1,0:T(8,128)(2,1)}, bf16[1344,256]{1,0:T(8,128)(2,1)}, u32[]{:S(2)}, u32[]{:S(2)}) collective-permute-start(bf16[1344,256]{1,0:T(8,128)(2,1)} %collective-permute-done.9.refs_2_.refs_4_), channel_id=1, source_target_pairs={{0,8},{4,12},{8,16},{12,20},{16,24},{20,28},{24,0},{28,4},{1,9},{5... | collective-permute-start | bytes 2064392 | tf_op jit(solution)/shard_map/ppermute | solution.py:109
  138.5 69.1 %collective-permute-start.20 = (bf16[1024,256]{1,0:T(8,128)(2,1)S(1)}, bf16[1024,256]{1,0:T(8,128)(2,1)}, u32[]{:S(2)}, u32[]{:S(2)}) collective-permute-start(bf16[1024,256]{1,0:T(8,128)(2,1)S(1)} %add_add_fusion.refs_3_.refs_10_), channel_id=1, source_target_pairs={{0,4},{4,0},{8,12},{12,8},{16,20},{20,16},{24,28},{28,24},{1,5},{5... | collective-permute-start | bytes 1572872 | tf_op jit(solution)/shard_map/ppermute | solution.py:21
  140.0 69.7 %collective-permute-start.21 = (bf16[1024,256]{1,0:T(8,128)(2,1)}, bf16[1024,256]{1,0:T(8,128)(2,1)}, u32[]{:S(2)}, u32[]{:S(2)}) collective-permute-start(bf16[1024,256]{1,0:T(8,128)(2,1)} %copy-done.22), channel_id=1, source_target_pairs={{0,4},{4,0},{8,12},{12,8},{16,20},{20,16},{24,28},{28,24},{1,5},{5... | collective-permute-start | bytes 1572872 | tf_op jit(solution)/shard_map/ppermute | solution.py:21
  152.7 55.4 %collective-permute-start.26 = (bf16[1024,256]{1,0:T(8,128)(2,1)}, bf16[1024,256]{1,0:T(8,128)(2,1)}, u32[]{:S(2)}, u32[]{:S(2)}) collective-permute-start(bf16[1024,256]{1,0:T(8,128)(2,1)} %collective-permute-done.25.refs_3_.refs_8_), channel_id=1, source_target_pairs={{0,8},{4,12},{8,16},{12,20},{16,24},{20,28},{24,0},{28,4},{1,9},{5... | collective-permute-start | bytes 1572872 | tf_op jit(solution)/shard_map/ppermute | solution.py:109
  153.1 56.9 %collective-permute-start.22 = (bf16[1024,256]{1,0:T(8,128)(2,1)}, bf16[1024,256]{1,0:T(8,128)(2,1)}, u32[]{:S(2)}, u32[]{:S(2)}) collective-permute-start(bf16[1024,256]{1,0:T(8,128)(2,1)} %collective-permute-done.18.refs_5_.refs_12_), channel_id=1, source_target_pairs={{0,4},{4,0},{8,12},{12,8},{16,20},{20,16},{24,28},{28,24},{1,5},{5... | collective-permute-start | bytes 1572872 | tf_op jit(solution)/shard_map/ppermute | solution.py:21
  161.4 50.4 %collective-permute-start.23 = (bf16[1024,256]{1,0:T(8,128)(2,1)S(1)}, bf16[1024,256]{1,0:T(8,128)(2,1)}, u32[]{:S(2)}, u32[]{:S(2)}) collective-permute-start(bf16[1024,256]{1,0:T(8,128)(2,1)S(1)} %collective-permute-done.19.refs_6_.refs_13_), channel_id=1, source_target_pairs={{0,4},{4,0},{8,12},{12,8},{16,20},{20,16},{24,28},{28,24},{1,5},{5... | collective-permute-start | bytes 1572872 | tf_op jit(solution)/shard_map/ppermute | solution.py:21
  207.6 38.4 %collective-permute-start.27 = (bf16[1024,256]{1,0:T(8,128)(2,1)}, bf16[1024,256]{1,0:T(8,128)(2,1)}, u32[]{:S(2)}, u32[]{:S(2)}) collective-permute-start(bf16[1024,256]{1,0:T(8,128)(2,1)} %refs_6_.1), channel_id=1, source_target_pairs={{0,4},{4,0},{8,12},{12,8},{16,20},{20,16},{24,28},{28,24},{1,5},{5... | collective-permute-start | bytes 1572872 | tf_op jit(solution)/shard_map/ppermute | solution.py:21
  208.0 38.0 %collective-permute-start.28 = (bf16[1024,256]{1,0:T(8,128)(2,1)}, bf16[1024,256]{1,0:T(8,128)(2,1)}, u32[]{:S(2)}, u32[]{:S(2)}) collective-permute-start(bf16[1024,256]{1,0:T(8,128)(2,1)} %collective-permute-done.24.refs_2_.refs_7_), channel_id=1, source_target_pairs={{0,4},{4,0},{8,12},{12,8},{16,20},{20,16},{24,28},{28,24},{1,5},{5... | collective-permute-start | bytes 1572872 | tf_op jit(solution)/shard_map/ppermute | solution.py:21
  209.7 36.3 %collective-permute-start.29 = (bf16[1024,256]{1,0:T(8,128)(2,1)}, bf16[1024,256]{1,0:T(8,128)(2,1)}, u32[]{:S(2)}, u32[]{:S(2)}) collective-permute-start(bf16[1024,256]{1,0:T(8,128)(2,1)} %collective-permute-done.25.refs_3_.refs_8_), channel_id=1, source_target_pairs={{0,4},{4,0},{8,12},{12,8},{16,20},{20,16},{24,28},{28,24},{1,5},{5... | collective-permute-start | bytes 1572872 | tf_op jit(solution)/shard_map/ppermute | solution.py:21
  210.1 46.0 %collective-permute-start.30 = (bf16[1024,256]{1,0:T(8,128)(2,1)}, bf16[1024,256]{1,0:T(8,128)(2,1)}, u32[]{:S(2)}, u32[]{:S(2)}) collective-permute-start(bf16[1024,256]{1,0:T(8,128)(2,1)} %collective-permute-done.26.refs_4_.refs_9_), channel_id=1, source_target_pairs={{0,4},{4,0},{8,12},{12,8},{16,20},{20,16},{24,28},{28,24},{1,5},{5... | collective-permute-start | bytes 1572872 | tf_op jit(solution)/shard_map/ppermute | solution.py:21
  362.8 62.3 %collective-permute-start.64 = (bf16[1024,256]{1,0:T(8,128)(2,1)}, bf16[1024,256]{1,0:T(8,128)(2,1)}, u32[]{:S(2)}, u32[]{:S(2)}) collective-permute-start(bf16[1024,256]{1,0:T(8,128)(2,1)} %get-tuple-element.148), channel_id=1, source_target_pairs={{0,4},{4,0},{8,12},{12,8},{16,20},{20,16},{24,28},{28,24},{1,5},{5... | collective-permute-start | bytes 1572872 | tf_op jit(solution)/shard_map/ppermute | solution.py:21
  363.5 81.3 %collective-permute-start.63 = (bf16[1024,256]{1,0:T(8,128)(2,1)}, bf16[1024,256]{1,0:T(8,128)(2,1)}, u32[]{:S(2)}, u32[]{:S(2)}) collective-permute-start(bf16[1024,256]{1,0:T(8,128)(2,1)} %get-tuple-element.149), channel_id=1, source_target_pairs={{0,4},{4,0},{8,12},{12,8},{16,20},{20,16},{24,28},{28,24},{1,5},{5... | collective-permute-start | bytes 1572872 | tf_op jit(solution)/shard_map/ppermute | solution.py:21
  368.6 59.9 %collective-permute-start.50 = (bf16[1024,256]{1,0:T(8,128)(2,1)}, bf16[1024,256]{1,0:T(8,128)(2,1)}, u32[]{:S(2)}, u32[]{:S(2)}) collective-permute-start(bf16[1024,256]{1,0:T(8,128)(2,1)} %get-tuple-element.152), channel_id=1, source_target_pairs={{0,4},{4,0},{8,12},{12,8},{16,20},{20,16},{24,28},{28,24},{1,5},{5... | collective-permute-start | bytes 1572872 | tf_op jit(solution)/shard_map/ppermute | solution.py:21
  369.4 86.8 %collective-permute-start.49 = (bf16[1024,256]{1,0:T(8,128)(2,1)}, bf16[1024,256]{1,0:T(8,128)(2,1)}, u32[]{:S(2)}, u32[]{:S(2)}) collective-permute-start(bf16[1024,256]{1,0:T(8,128)(2,1)} %get-tuple-element.153), channel_id=1, source_target_pairs={{0,4},{4,0},{8,12},{12,8},{16,20},{20,16},{24,28},{28,24},{1,5},{5... | collective-permute-start | bytes 1572872 | tf_op jit(solution)/shard_map/ppermute | solution.py:21
  425.1 40.1 %collective-permute-start.32 = (bf16[256,2048]{1,0:T(8,128)(2,1)}, bf16[256,2048]{1,0:T(8,128)(2,1)}, u32[]{:S(2)}, u32[]{:S(2)}) collective-permute-start(bf16[256,2048]{1,0:T(8,128)(2,1)} %get-tuple-element.142), channel_id=1, source_target_pairs={{0,1},{1,0},{2,3},{3,2},{4,5},{5,4},{6,7},{7,6},{8,9},{9,8},{10,11... | collective-permute-start | bytes 3145736 | tf_op jit(solution)/shard_map/ppermute | solution.py:21
  444.8 42.5 %collective-permute-start.62 = (bf16[1024,256]{1,0:T(8,128)(2,1)}, bf16[1024,256]{1,0:T(8,128)(2,1)S(1)}, u32[]{:S(2)}, u32[]{:S(2)}) collective-permute-start(bf16[1024,256]{1,0:T(8,128)(2,1)} %get-tuple-element.150), channel_id=1, source_target_pairs={{0,4},{4,0},{8,12},{12,8},{16,20},{20,16},{24,28},{28,24},{1,5},{5... | collective-permute-start | bytes 1572872 | tf_op jit(solution)/shard_map/ppermute | solution.py:21
  453.6 49.8 %collective-permute-start.48 = (bf16[1024,256]{1,0:T(8,128)(2,1)}, bf16[1024,256]{1,0:T(8,128)(2,1)S(1)}, u32[]{:S(2)}, u32[]{:S(2)}) collective-permute-start(bf16[1024,256]{1,0:T(8,128)(2,1)} %get-tuple-element.154), channel_id=1, source_target_pairs={{0,4},{4,0},{8,12},{12,8},{16,20},{20,16},{24,28},{28,24},{1,5},{5... | collective-permute-start | bytes 1572872 | tf_op jit(solution)/shard_map/ppermute | solution.py:21
  488.6 39.8 %collective-permute-start.45 = (bf16[1344,256]{1,0:T(8,128)(2,1)S(1)}, bf16[1344,256]{1,0:T(8,128)(2,1)S(1)}, u32[]{:S(2)}, u32[]{:S(2)}) collective-permute-start(bf16[1344,256]{1,0:T(8,128)(2,1)S(1)} %add_convert_fusion.1), channel_id=1, source_target_pairs={{0,8},{4,12},{8,16},{12,20},{16,24},{20,28},{24,0},{28,4},{1,9},{5... | collective-permute-start | bytes 2064392 | tf_op jit(solution)/shard_map/ppermute | solution.py:135
  503.5 37.4 %collective-permute-start.47 = (bf16[1024,256]{1,0:T(8,128)(2,1)S(1)}, bf16[1024,256]{1,0:T(8,128)(2,1)S(1)}, u32[]{:S(2)}, u32[]{:S(2)}) collective-permute-start(bf16[1024,256]{1,0:T(8,128)(2,1)S(1)} %copy-done.40), channel_id=1, source_target_pairs={{0,4},{4,0},{8,12},{12,8},{16,20},{20,16},{24,28},{28,24},{1,5},{5... | collective-permute-start | bytes 1572872 | tf_op jit(solution)/shard_map/ppermute | solution.py:21
  513.7 36.4 %collective-permute-start.31 = (bf16[256,2048]{1,0:T(8,128)(2,1)S(1)}, bf16[256,2048]{1,0:T(8,128)(2,1)S(1)}, u32[]{:S(2)}, u32[]{:S(2)}) collective-permute-start(bf16[256,2048]{1,0:T(8,128)(2,1)S(1)} %copy-done.29), channel_id=1, source_target_pairs={{0,1},{1,0},{2,3},{3,2},{4,5},{5,4},{6,7},{7,6},{8,9},{9,8},{10,11... | collective-permute-start | bytes 3145736 | tf_op jit(solution)/shard_map/ppermute | solution.py:21
  540.8 35.8 %collective-permute-start.40 = (bf16[1344,256]{1,0:T(8,128)(2,1)S(1)}, bf16[1344,256]{1,0:T(8,128)(2,1)S(1)}, u32[]{:S(2)}, u32[]{:S(2)}) collective-permute-start(bf16[1344,256]{1,0:T(8,128)(2,1)S(1)} %copy-done.32), channel_id=1, source_target_pairs={{0,4},{4,0},{8,12},{12,8},{16,20},{20,16},{24,28},{28,24},{1,5},{5... | collective-permute-start | bytes 2064392 | tf_op jit(solution)/shard_map/ppermute | solution.py:21
  (107 other events, 2325.0 us)
where the time goes:
time: 607 us; the launch traced here: 601 us
  waiting for transfers between devices  217 us (36%)
  Pallas kernels  175 us (29%)
  starting transfers between devices  81.9 us (13%)
  local copies, waits for them, and re-layouts  43 us (7%)
  other arithmetic  41.6 us (7%)
  matrix products  27.8 us (5%)
  blocking collectives  11.9 us (2%)
    ppermute x41, waiting for transfers between devices, flip(): lax.ppermute(value, axis, [(i, i ^ bit) for i in range(lax.axis_size(axis...  71.7 us
    pallas_call x4, Pallas kernels, run_scan_backward(): pl.pallas_call(functools.partial(scan_backward, held is None, at == 0), g...  66.1 us
    ppermute x9, waiting for transfers between devices, gather_dp(): mine.append(lax.ppermute(mine[step], 'dp', ring))  64.7 us
    ppermute x9, waiting for transfers between devices, scatter_dp(): carried = lax.ppermute(total.astype(BF16), 'dp', ring)  61.6 us
    ppermute x41, starting transfers between devices, flip(): lax.ppermute(value, axis, [(i, i ^ bit) for i in range(lax.axis_size(axis...  48.6 us
    pallas_call x2, Pallas kernels, run_products(): pl.pallas_call(kernel, grid=(rows // TALL,), in_specs=[tall_spec(left) fo...  29.4 us
    dot_general x6, matrix products, multiply(): lax.dot_general(left, some, (((0,), (0,)), ((), ())), preferred_element_t...  27.8 us
    pallas_call x2, Pallas kernels, run_scan_forward(): pl.pallas_call(functools.partial(scan_forward, held is None), grid=(per,)...  21.8 us
  transfers between devices with their start and end apart: 73, of which 25 were waited for; matrix products, arithmetic and copies ran while one was open for 15% of the time, Pallas kernels for 15%

commit v1 on v0

--- a/solution.py
+++ b/solution.py
@@ -15,6 +15,8 @@
 EPSILON = 1e-05
 F32 = jnp.float32
 BF16 = jnp.bfloat16
+DP, STATE = "dp", "state"
+IN_ORDER = pltpu.CompilerParams(dimension_semantics=("arbitrary",))
 
 
 def flip(value, axis, bit):
@@ -49,12 +51,12 @@
 
 
 def gather_state(own):
-    count, here = lax.axis_size("state"), lax.axis_index("state")
+    count, here = lax.axis_size(STATE), lax.axis_index(STATE)
     held = {0: own}
     bit = count // 2
     while bit:
         for key in list(held):
-            held[key | bit] = flip(held[key], "state", bit)
+            held[key | bit] = flip(held[key], STATE, bit)
         bit //= 2
     keys = sorted(held)
     return stack_rows([held[key] for key in keys], here ^ jnp.array(keys))
@@ -98,26 +100,26 @@
 
 
 def gather_dp(own):
-    count = lax.axis_size("dp")
-    if not ringed("dp"):
-        return [lax.all_gather(own, "dp", axis=1, tiled=True)]
+    count = lax.axis_size(DP)
+    if not ringed(DP):
+        return [lax.all_gather(own, DP, axis=1, tiled=True)]
     ring = [(i, (i + 2) % count) for i in range(count)]
     mine, other = [own], []
     for step in range(count // 2):
-        other.append(flip(mine[step], "dp", 1))
+        other.append(flip(mine[step], DP, 1))
         if step + 1 < count // 2:
-            mine.append(lax.ppermute(mine[step], "dp", ring))
+            mine.append(lax.ppermute(mine[step], DP, ring))
     return mine + other
 
 
 def scatter_dp(left, right):
-    count = lax.axis_size("dp")
+    count = lax.axis_size(DP)
 
     def multiply(some, kind):
         return lax.dot_general(left, some, (((0,), (0,)), ((), ())), preferred_element_type=kind)
 
-    if not ringed("dp"):
-        return lax.psum_scatter(multiply(right, F32), "dp", scatter_dimension=1, tiled=True)
+    if not ringed(DP):
+        return lax.psum_scatter(multiply(right, F32), DP, scatter_dimension=1, tiled=True)
     steps = count // 2
     half = right.shape[1] // 2
     wide = half // steps
@@ -127,23 +129,23 @@
     carried = None
     for step in range(1, steps + 1):
         at = step % steps * wide
-        came = flip(other[:, at : at + wide], "dp", 1)
+        came = flip(other[:, at : at + wide], DP, 1)
         total = mine[:, at : at + wide].astype(F32) + came.astype(F32)
         if carried is not None:
             total = total + carried.astype(F32)
         if step < steps:
-            carried = lax.ppermute(total.astype(BF16), "dp", ring)
+            carried = lax.ppermute(total.astype(BF16), DP, ring)
     return total
 
 
 def scatter_state(whole):
-    count, here = lax.axis_size("state"), lax.axis_index("state")
+    count, here = lax.axis_size(STATE), lax.axis_index(STATE)
     rows = whole.reshape(count, whole.shape[0] // count, whole.shape[1])
     parts = {key: lax.dynamic_index_in_dim(rows, here ^ key, 0, keepdims=False) for key in range(count)}
     bit = 1
     while bit < count:
         for key in [k for k in parts if not k & bit]:
-            sent = flip(parts.pop(key | bit).astype(BF16), "state", bit)
+            sent = flip(parts.pop(key | bit).astype(BF16), STATE, bit)
             parts[key] = parts[key].astype(F32) + sent.astype(F32)
         bit *= 2
     return parts[0]
@@ -189,7 +191,7 @@
         in_specs=[pl.BlockSpec(memory_space=pltpu.SMEM), pl.BlockSpec(memory_space=pltpu.VMEM)],
         out_specs=[pl.BlockSpec(memory_space=pltpu.VMEM) for _ in plans],
         out_shape=[jax.ShapeDtypeStruct((size, width), BF16) for size in sizes],
-        name="cut_rows",
+        name="cut",
     )(group[None], own)
 
 
@@ -221,7 +223,7 @@
         + [pl.BlockSpec(memory_space=pltpu.VMEM) for _ in pieces],
         out_specs=pl.BlockSpec(memory_space=pltpu.VMEM),
         out_shape=jax.ShapeDtypeStruct((store, width), F32),
-        name="paste_rows",
+        name="paste",
     )(group[None], *pieces)
 
 
@@ -505,8 +507,8 @@
         out_specs=tall_spec(out),
         out_shape=out,
         scratch_shapes=[joined(pieces)],
-        compiler_params=pltpu.CompilerParams(dimension_semantics=("arbitrary",)),
-        name="project",
+        compiler_params=IN_ORDER,
+        name="pj",
     )(left, *pieces)
 
 
@@ -543,7 +545,7 @@
             + [whole_spec(c) for c in carried],
             out_shape=outs + carried,
             input_output_aliases=aliases,
-            compiler_params=pltpu.CompilerParams(dimension_semantics=("arbitrary",)),
+            compiler_params=IN_ORDER,
         )(*args)
     return held[:3]
 
@@ -578,8 +580,8 @@
         out_specs=[tall_spec(mixed), across_spec()],
         out_shape=[jax.ShapeDtypeStruct((rows, cols), BF16), jax.ShapeDtypeStruct((8, rows), F32)],
         scratch_shapes=[joined(pieces)],
-        compiler_params=pltpu.CompilerParams(dimension_semantics=("arbitrary",)),
-        name="gate_forward",
+        compiler_params=IN_ORDER,
+        name="gf",
     )(normed, mixed, mask, *pieces)
 
 
@@ -596,7 +598,7 @@
         in_specs=[row_spec(mixed), row_spec(gate), row_spec(scale), whole_spec(gain)],
         out_specs=row_spec(gate),
         out_shape=jax.ShapeDtypeStruct(gate.shape, BF16),
-        name="normalize",
+        name="nr",
     )(mixed, gate, scale, gain)
 
 
@@ -631,50 +633,47 @@
             jax.ShapeDtypeStruct((1, cols), F32),
         ],
         scratch_shapes=[joined(pieces)],
-        compiler_params=pltpu.CompilerParams(dimension_semantics=("arbitrary",)),
-        name="gate_backward",
+        compiler_params=IN_ORDER,
+        name="gb",
     )(cot, mixed, gate, scale, gain, mask, *pieces)
 
 
-def run_products(lefts, piece_lists, against=None):
-    rows = lefts[0].shape[0]
-    count = len(lefts)
-    number = len(piece_lists[0])
-    wide = piece_lists[0][0].shape[1]
-    flat = [piece for pieces in piece_lists for piece in pieces]
-    others = [] if against is None else [against]
-
-    def kernel(*refs):
-        wholes = refs[-count:]
-        other = refs[count + len(flat) : -count]
-        total = None
-        for at in range(count):
-            join(refs[count + at * number : count + (at + 1) * number], wholes[at])
-            part = dots(refs[at][...], wholes[at][...], ((1,), (0,)))
-            total = part if total is None else total + part
-        other[len(others)][...] = total.astype(BF16)
+def run_products(left, pieces, onto=None, against=None):
+    rows = left.shape[0]
+    others = [] if onto is None else [onto, against]
+
+    def kernel(left_ref, *refs):
+        join(refs[: len(pieces)], refs[-1])
+        total = dots(left_ref[...], refs[-1][...], ((1,), (0,)))
         if others:
-            sums = jnp.sum(total * other[0][...].astype(F32), axis=0, keepdims=True)
+            onto_ref, against_ref, out_ref, sums_ref = refs[len(pieces) : -1]
+            total = total + onto_ref[...].astype(F32)
+            sums = jnp.sum(total * against_ref[...].astype(F32), axis=0, keepdims=True)
 
             @pl.when(pl.program_id(0) == 0)
             def _():
-                other[2][...] = sums
+                sums_ref[...] = sums
 
             @pl.when(pl.program_id(0) > 0)
             def _():
-                other[2][...] += sums
-
-    out = jax.ShapeDtypeStruct((rows, wide * number), BF16)
-    sums = [jax.ShapeDtypeStruct((1, wide * number), F32)] * len(others)
+                sums_ref[...] += sums
+
+        else:
+            out_ref = refs[-2]
+        out_ref[...] = total.astype(BF16)
+
+    whole = joined(pieces)
+    out = jax.ShapeDtypeStruct((rows, whole.shape[1]), BF16)
+    sums = [jax.ShapeDtypeStruct((1, whole.shape[1]), F32)] if others else []
     return pl.pallas_call(
         kernel,
         grid=(rows // TALL,),
-        in_specs=[tall_spec(left) for left in lefts] + [whole_spec(p) for p in flat] + [tall_spec(o) for o in others],
+        in_specs=[tall_spec(left)] + [whole_spec(p) for p in pieces] + [tall_spec(o) for o in others],
         out_specs=[tall_spec(out)] + [whole_spec(total) for total in sums],
         out_shape=[out] + sums,
-        scratch_shapes=[joined(pieces) for pieces in piece_lists],
-        compiler_params=pltpu.CompilerParams(dimension_semantics=("arbitrary",)),
-    )(*lefts, *flat, *others)
+        scratch_shapes=[whole],
+        compiler_params=IN_ORDER,
+    )(left, *pieces, *others)
 
 
 def run_scan_backward(x_proj, act, mixed_low, starts, params):
@@ -742,7 +741,7 @@
     inner = H * P_SIZE
     xbc = inner + 2 * N
     full_cols = 2 * inner + 2 * N + H
-    groups, group = lax.axis_size("state"), lax.axis_index("state")
+    groups, group = lax.axis_size(STATE), lax.axis_index(STATE)
     seq_rows = tok_rows * groups
     heads = H // groups
     cols = inner // groups
@@ -771,13 +770,13 @@
         return [ranges(g + shift) if 0 <= g + shift < groups else None for g in range(groups)]
 
     kinds = (("v", value_range, value_moves), ("b", tail_range, tail_moves), ("g", gate_range, gate_moves))
-    sends = [(f"{kind}{abs(shift)}", ranges, shift, found[shift]) for kind, ranges, found in kinds for shift in sorted(found)]
+    sends = [(kind + str(abs(shift)), ranges, shift, found[shift]) for kind, ranges, found in kinds for shift in sorted(found)]
     plans = [at_shift(x_ranges, 0), at_shift(lambda i: [gate_range(i)], 0)]
     plans += [at_shift(lambda i, ranges=ranges: [ranges(i)], shift) for _, ranges, shift, _ in sends]
     w_x_own, w_g_own, *cuts = cut_rows(w_in.T, group, plans)
     came = {"v": None, "b": None, "g": None}
     for (name, _, _, found), cut in zip(sends, cuts):
-        part = lax.ppermute(cut, "state", found)
+        part = lax.ppermute(cut, STATE, found)
         came[name[0]] = part if came[name[0]] is None else came[name[0]] + part
     w_x_own = w_x_own + jnp.concatenate([came["v"], came["b"]], axis=0)
     w_g_own = w_g_own + came["g"]
@@ -787,9 +786,9 @@
     normed = (tokens * in_scale * norm_in_gain).astype(BF16)
 
     w_x = gather_dp(w_x_own)
-    normed_all = gather_state(to_ring(normed, "dp"))
+    normed_all = gather_state(to_ring(normed, DP))
     w_g = gather_dp(w_g_own)
-    cot_all = gather_state(to_ring(out_cotangent, "dp"))
+    cot_all = gather_state(to_ring(out_cotangent, DP))
     w_o = gather_dp(w_out)
 
     own_heads = heads * group
@@ -813,7 +812,7 @@
     active = (heads_on * P_SIZE).astype(F32)
     gain_mask = gain_own[None] * mask
     gate, square = run_gate(normed_all, mixed, mask, w_g)
-    square = lax.psum(square[:1], "state")
+    square = lax.psum(square[:1], STATE)
     scale_row = lax.rsqrt(square / active + EPSILON)
     out_scale = scale_row.reshape(seq_rows, 1)
     normed_out = run_normalize(mixed, gate, out_scale, gain_mask)
@@ -826,14 +825,14 @@
     gate_sig = jax.nn.sigmoid(gate_f)
     gate_act = gate_f * gate_sig
     gated = mixed * gate_act
-    aligned = lax.psum(aligned[:1], "state").reshape(seq_rows, 1)
+    aligned = lax.psum(aligned[:1], STATE).reshape(seq_rows, 1)
     pull = (aligned / active) * out_scale * out_scale * out_scale
     gated_grad = out_grad * gain_mask * out_scale - gated * mask * pull
     mixed_grad = gated_grad * gate_act
     gate_grad = (gated_grad * mixed * (gate_sig * (1.0 + gate_f * (1.0 - gate_sig)))).astype(BF16)
 
-    (out_whole,) = run_products([normed_out], [w_o])
-    block_out = (tokens + from_ring(scatter_state(out_whole), "dp")).astype(BF16)
+    (out_whole,) = run_products(normed_out, w_o)
+    block_out = (tokens + from_ring(scatter_state(out_whole), DP)).astype(BF16)
     grad_in_gate = scatter_dp(gate_grad, normed_all)
     x_grad, conv_sums, skip_sums, head_sums = run_scan_backward(
         x_proj, act, mixed_grad.astype(BF16), starts, scan_params
@@ -848,18 +847,19 @@
     pieces = [grad_in_x, grad_in_gate]
     plans = [at_shift(x_ranges, 0), at_shift(lambda i: [gate_range(i)], 0)]
     for name, ranges, shift, found in sends:
-        pieces.append(lax.ppermute(held[name[0]], "state", [(b, a) for a, b in found]))
+        pieces.append(lax.ppermute(held[name[0]], STATE, [(b, a) for a, b in found]))
         plans.append(at_shift(lambda i, ranges=ranges: [ranges(i)], shift))
     grad_in_proj = paste_rows(pieces, group, plans, store).T
 
-    normed_whole, gain_sums = run_products([x_grad, gate_grad], [w_x, w_g], normed_all)
-    normed_grad = from_ring(scatter_state(normed_whole), "dp")
+    (normed_x,) = run_products(x_grad, w_x)
+    normed_whole, gain_sums = run_products(gate_grad, w_g, normed_x, normed_all)
+    normed_grad = from_ring(scatter_state(normed_whole), DP)
     pushed = normed_grad * norm_in_gain
     token_grad = in_scale * pushed - tokens * (
         in_scale * in_scale * in_scale * jnp.mean(pushed * tokens, axis=-1, keepdims=True)
     )
     grad_input = out_cotangent.astype(F32) + token_grad
-    grad_norm_in = from_ring(gain_sums, "dp")[0] / norm_in_gain
+    grad_norm_in = from_ring(gain_sums, DP)[0] / norm_in_gain
 
     def spread(entries, total, at):
         return lax.dynamic_update_slice_in_dim(
@@ -880,7 +880,7 @@
     sizes = [entry.shape[0] for entry in flat]
     packed = jnp.concatenate(flat)
     packed = jnp.pad(packed, (0, -packed.shape[0] % 1024)).reshape(-1, 128)
-    packed = sum_axis(sum_axis(packed, "state"), "dp").reshape(-1)
+    packed = sum_axis(sum_axis(packed, STATE), DP).reshape(-1)
     summed = []
     at = 0
     for size in sizes:
@@ -902,9 +902,9 @@
 
 
 def solution(mesh):
-    rows = P(("dp", "state"), None)
+    rows = P((DP, STATE), None)
     whole = P()
-    in_specs = (rows, P("dp"), P("dp", "state"), P("state", "dp")) + (whole,) * 7 + (rows,)
-    out_specs = (rows, rows, P("dp", "state"), P("state", "dp")) + (whole,) * 7
+    in_specs = (rows, P(DP), P(DP, STATE), P(STATE, DP)) + (whole,) * 7 + (rows,)
+    out_specs = (rows, rows, P(DP, STATE), P(STATE, DP)) + (whole,) * 7
 
     return jax.shard_map(local, mesh=mesh, in_specs=in_specs, out_specs=out_specs, check_vma=False)

time: 607 us -> 612 us (level)
    pallas_call x2 -> x3, Pallas kernels: 29.4 us -> 33.6 us  [run_products(): pl.pallas_call(kernel, grid=(rows // TALL,), in_specs=[tall_spec(left)] +...]
where the time goes in v1:
time: 612 us; the launch traced here: 606 us
  waiting for transfers between devices  217 us (35%)
  Pallas kernels  179 us (29%)
  starting transfers between devices  81.8 us (13%)
  local copies, waits for them, and re-layouts  43.1 us (7%)
  other arithmetic  41.7 us (7%)
  matrix products  27.7 us (5%)
  blocking collectives  11.9 us (2%)
    ppermute x41, waiting for transfers between devices, flip(): lax.ppermute(value, axis, [(i, i ^ bit) for i in range(lax.axis_size(axis...  72.1 us
    pallas_call x4, Pallas kernels, run_scan_backward(): pl.pallas_call(functools.partial(scan_backward, held is None, at == 0), g...  66.1 us
    ppermute x9, waiting for transfers between devices, gather_dp(): mine.append(lax.ppermute(mine[step], DP, ring))  64.7 us
    ppermute x9, waiting for transfers between devices, scatter_dp(): carried = lax.ppermute(total.astype(BF16), DP, ring)  61.4 us
    ppermute x41, starting transfers between devices, flip(): lax.ppermute(value, axis, [(i, i ^ bit) for i in range(lax.axis_size(axis...  48.6 us
    pallas_call x3, Pallas kernels, run_products(): pl.pallas_call(kernel, grid=(rows // TALL,), in_specs=[tall_spec(left)] +...  33.6 us
    dot_general x6, matrix products, multiply(): lax.dot_general(left, some, (((0,), (0,)), ((), ())), preferred_element_t...  27.7 us
    pallas_call x2, Pallas kernels, run_scan_forward(): pl.pallas_call(functools.partial(scan_forward, held is None), grid=(per,)...  21.8 us
  transfers between devices with their start and end apart: 73, of which 25 were waited for; matrix products, arithmetic and copies ran while one was open for 15% of the time, Pallas kernels for 15%

profile of v1, /device:TPU:0, one launch (start us, length us, event | category | flops | bytes accessed | tf_op | source)
XLA Modules:
  0.0 605.6 jit_solution(6992893172662294832)
XLA Ops:
  38.5 9.6 %collective-permute-done.24.refs_1_.refs_7_ = bf16[1024,256]{1,0:T(8,128)(2,1)} collective-permute-done((bf16[1024,256]{1,0:T(8,128)(2,1)}, bf16[1024,256]{1,0:T(8,128)(2,1)}, u32[]{:S(2)}, u32[]{:S(2)}) %collective-permute-start.24) | collective-permute-done | bytes 524320 | tf_op jit(solution)/shard_map/ppermute | solution.py:111
  51.6 13.3 %collective-permute-done.16 = bf16[1024,256]{1,0:T(8,128)(2,1)S(1)} collective-permute-done((bf16[1024,256]{1,0:T(8,128)(2,1)S(1)}, bf16[1024,256]{1,0:T(8,128)(2,1)S(1)}, u32[]{:S(2)}, u32[]{:S(2)}) %collective-permute-start.16) | collective-permute-done | bytes 524320 | tf_op jit(solution)/shard_map/ppermute | solution.py:779
  81.4 9.9 %collective-permute-done.9.refs_2_ = bf16[1344,256]{1,0:T(8,128)(2,1)} collective-permute-done((bf16[1344,256]{1,0:T(8,128)(2,1)S(1)}, bf16[1344,256]{1,0:T(8,128)(2,1)}, u32[]{:S(2)}, u32[]{:S(2)}) %collective-permute-start.9) | collective-permute-done | bytes 688160 | tf_op jit(solution)/shard_map/ppermute | solution.py:111
  91.3 11.1 %collective-permute-done.17.refs_4_.refs_1_ = bf16[1024,256]{1,0:T(8,128)(2,1)S(1)} collective-permute-done((bf16[1024,256]{1,0:T(8,128)(2,1)S(1)}, bf16[1024,256]{1,0:T(8,128)(2,1)S(1)}, u32[]{:S(2)}, u32[]{:S(2)}) %collective-permute-start.17) | collective-permute-done | bytes 524320 | tf_op jit(solution)/shard_map/ppermute | solution.py:111
  108.8 19.7 %collective-permute-done.18.refs_5_.refs_2_ = bf16[1024,256]{1,0:T(8,128)(2,1)} collective-permute-done((bf16[1024,256]{1,0:T(8,128)(2,1)S(1)}, bf16[1024,256]{1,0:T(8,128)(2,1)}, u32[]{:S(2)}, u32[]{:S(2)}) %collective-permute-start.18) | collective-permute-done | bytes 524320 | tf_op jit(solution)/shard_map/ppermute | solution.py:111
  140.6 12.1 %collective-permute-done.19.refs_6_.refs_3_ = bf16[1024,256]{1,0:T(8,128)(2,1)S(1)} collective-permute-done((bf16[1024,256]{1,0:T(8,128)(2,1)}, bf16[1024,256]{1,0:T(8,128)(2,1)S(1)}, u32[]{:S(2)}, u32[]{:S(2)}) %collective-permute-start.19) | collective-permute-done | bytes 524320 | tf_op jit(solution)/shard_map/ppermute | solution.py:111
  173.9 12.0 %pj.1.refs_0_.refs_1_ = bf16[1024,1344]{1,0:T(8,128)(2,1)} custom-call(bf16[1024,2048]{1,0:T(8,128)(2,1)} %shard_map.221.left_ref.refs_0_.refs_9_, bf16[1344,256]{1,0:T(8,128)(2,1)} %copy-done.12, bf16[1344,256]{1,0:T(8,128)(2,1)} %copy-done.19, bf16[1344,256]{1,0:T(8,128)(2,1)} %collective-permute-done.9.refs_2_, ...), custom_call_target="tpu_custom_call" | custom-call | tf_op jit(solution)/shard_map/pj/pallas_call | solution.py:503
  185.9 10.8 %shard_map.222 = (bf16[1024,1280]{1,0:T(8,128)(2,1)}, f32[1024,1024]{1,0:T(8,128)}, f32[4096,128]{1,0:T(8,128)}, f32[8,1280]{1,0:T(8,128)}, f32[1024,128]{1,0:T(8,128)}) custom-call(bf16[1024,1344]{1,0:T(8,128)(2,1)} %pj.1.refs_0_.refs_1_, f32[4,1280]{1,0:T(4,128)} %pad_maximum_fusion.2.refs_1_.refs_5_, f32[1,1280]{1,0:T(1,128)} %broadcast_in_dim.40.refs_2_.refs_6_, ...), custom_call_target="tpu_custom_call" | custom-call | tf_op jit(solution)/shard_map/pallas_call | solution.py:536
  196.7 11.0 %shard_map.223 = (bf16[1024,1280]{1,0:T(8,128)(2,1)}, f32[1024,1024]{1,0:T(8,128)}, f32[4096,128]{1,0:T(8,128)}, f32[8,1280]{1,0:T(8,128)}, f32[1024,128]{1,0:T(8,128)}) custom-call(bf16[1024,1344]{1,0:T(8,128)(2,1)} %pj.1.refs_0_.refs_1_, ...), custom_call_target="tpu_custom_call", output_to_operand_aliasing={{0}: (9, {}), {1}: (10, {}), {2}: (11, {}), {3}: (12, {}), ... | custom-call | tf_op jit(solution)/shard_map/pallas_call | solution.py:536
  211.9 11.0 %gf.1 = (bf16[1024,1024]{1,0:T(8,128)(2,1)}, f32[8,1024]{1,0:T(8,128)}) custom-call(bf16[1024,2048]{1,0:T(8,128)(2,1)} %shard_map.221.left_ref.refs_0_.refs_9_, f32[1024,1024]{1,0:T(8,128)} %get-tuple-element.103.refs_1_.mixed_ref, f32[1,1024]{1,0:T(1,128)} %compare_convert_fusion.refs_2_.refs_5_, bf16[1024,256]{1,0:T(8,128)(2,1)} %copy-done.13, ...), custom_call_target="tpu_custom_call" | custom-call | tf_op jit(solution)/shard_map/gf/pallas_call | solution.py:576
  246.1 10.1 %collective-permute-done.30.refs_7_.refs_13_ = bf16[1024,256]{1,0:T(8,128)(2,1)} collective-permute-done((bf16[1024,256]{1,0:T(8,128)(2,1)}, bf16[1024,256]{1,0:T(8,128)(2,1)}, u32[]{:S(2)}, u32[]{:S(2)}) %collective-permute-start.30) | collective-permute-done | bytes 524320 | tf_op jit(solution)/shard_map/ppermute | solution.py:23
  256.1 12.6 %gb.1 = (f32[1024,1024]{1,0:T(8,128)}, f32[8,1024]{1,0:T(8,128)}, f32[1,1024]{1,0:T(1,128)}) custom-call(bf16[1024,2048]{1,0:T(8,128)(2,1)} %shard_map.225.refs_0_, f32[1024,1024]{1,0:T(8,128)} %get-tuple-element.103.refs_1_.mixed_ref, bf16[1024,1024]{1,0:T(8,128)(2,1)} %get-tuple-element.104.gate_ref.refs_2_, f32[1024,1]{1,0:T(8,128)} %copy.64.scale_ref.refs_3_, ...), custom_call_target="tpu_custom_call" | custom-call | tf_op jit(solution)/shard_map/gb/pallas_call | solution.py:623
  282.2 16.2 %shard_map.226 = (bf16[1024,1344]{1,0:T(8,128)(2,1)}, f32[8,1280]{1,0:T(8,128)}, f32[1024,128]{1,0:T(8,128)}, f32[8,1280]{1,0:T(8,128)}, f32[1,1024]{1,0:T(1,128)}, /*index=5*/f32[8,16]{1,0:T(8,128)}) custom-call(bf16[1024,1344]{1,0:T(8,128)(2,1)} %pj.1.refs_0_.refs_1_, bf16[1024,1344]{1,0:T(8,128)(2,1)} %pj.1.refs_0_.refs_1_, ...), custom_call_target="tpu_custom_call" | custom-call | tf_op jit(solution)/shard_map/pallas_call | solution.py:707
  298.5 16.6 %shard_map.227 = (bf16[1024,1344]{1,0:T(8,128)(2,1)}, f32[8,1280]{1,0:T(8,128)}, f32[1024,128]{1,0:T(8,128)}, f32[8,1280]{1,0:T(8,128)}, f32[1,1024]{1,0:T(1,128)}, /*index=5*/f32[8,16]{1,0:T(8,128)}) custom-call(bf16[1024,1344]{1,0:T(8,128)(2,1)} %pj.1.refs_0_.refs_1_, ...), custom_call_target="tpu_custom_call", output_to_operand_aliasing={{0}: (13, {}), {1}: (14, {}), {2}: (15, {}), {3}: (16, {}),... | custom-call | tf_op jit(solution)/shard_map/pallas_call | solution.py:707
  315.1 16.8 %shard_map.228 = (bf16[1024,1344]{1,0:T(8,128)(2,1)}, f32[8,1280]{1,0:T(8,128)}, f32[1024,128]{1,0:T(8,128)}, f32[8,1280]{1,0:T(8,128)}, f32[1,1024]{1,0:T(1,128)}, /*index=5*/f32[8,16]{1,0:T(8,128)}) custom-call(bf16[1024,1344]{1,0:T(8,128)(2,1)} %pj.1.refs_0_.refs_1_, ...), custom_call_target="tpu_custom_call", output_to_operand_aliasing={{0}: (13, {}), {1}: (14, {}), {2}: (15, {}), {3}: (16, {}),... | custom-call | tf_op jit(solution)/shard_map/pallas_call | solution.py:707
  331.9 16.5 %shard_map.229 = (bf16[1024,1344]{1,0:T(8,128)(2,1)}, f32[8,1280]{1,0:T(8,128)}, f32[1024,128]{1,0:T(8,128)}, f32[8,1280]{1,0:T(8,128)}, f32[1,1024]{1,0:T(1,128)}, /*index=5*/f32[8,16]{1,0:T(8,128)}) custom-call(bf16[1024,1344]{1,0:T(8,128)(2,1)} %pj.1.refs_0_.refs_1_, ...), custom_call_target="tpu_custom_call", output_to_operand_aliasing={{0}: (13, {}), {1}: (14, {}), {2}: (15, {}), {3}: (16, {}),... | custom-call | tf_op jit(solution)/shard_map/pallas_call | solution.py:707
  373.7 12.4 %shard_map.230.refs_8_ = bf16[1024,2048]{1,0:T(8,128)(2,1)} custom-call(bf16[1024,1344]{1,0:T(8,128)(2,1)} %get-tuple-element.126.left_ref, bf16[1344,256]{1,0:T(8,128)(2,1)} %copy-done.12, bf16[1344,256]{1,0:T(8,128)(2,1)} %copy-done.19, bf16[1344,256]{1,0:T(8,128)(2,1)} %collective-permute-done.9.refs_2_, ...), custom_call_target="tpu_custom_call" | custom-call | tf_op jit(solution)/shard_map/pallas_call | solution.py:668
  386.0 11.9 %shard_map.231 = (bf16[1024,2048]{1,0:T(8,128)(2,1)}, f32[1,2048]{1,0:T(1,128)}) custom-call(bf16[1024,1024]{1,0:T(8,128)(2,1)} %get-tuple-element.138.left_ref, bf16[1024,256]{1,0:T(8,128)(2,1)} %copy-done.13, bf16[1024,256]{1,0:T(8,128)(2,1)} %copy-done.22, bf16[1024,256]{1,0:T(8,128)(2,1)} %collective-permute-done.18.refs_5_.refs_2_, ...), custom_call_target="tpu_custom_call" | custom-call | tf_op jit(solution)/shard_map/pallas_call | solution.py:668
  409.2 9.3 %shard_map.224 = bf16[1024,2048]{1,0:T(8,128)(2,1)} custom-call(bf16[1024,1024]{1,0:T(8,128)(2,1)} %nr.1.left_ref, bf16[1024,256]{1,0:T(8,128)(2,1)} %refs_6_.1, bf16[1024,256]{1,0:T(8,128)(2,1)} %collective-permute-done.24.refs_1_.refs_7_, bf16[1024,256]{1,0:T(8,128)(2,1)} %collective-permute-done.25.refs_2_.refs_8_, ...), custom_call_target="tpu_custom_call" | custom-call | tf_op jit(solution)/shard_map/pallas_call | solution.py:668
  471.2 17.7 %collective-permute-done.42 = bf16[1344,256]{1,0:T(8,128)(2,1)S(1)} collective-permute-done((bf16[1344,256]{1,0:T(8,128)(2,1)}, bf16[1344,256]{1,0:T(8,128)(2,1)S(1)}, u32[]{:S(2)}, u32[]{:S(2)}) %collective-permute-start.42) | collective-permute-done | bytes 688160 | tf_op jit(solution)/shard_map/ppermute | solution.py:23
  496.8 10.0 %collective-permute-done.66 = bf16[1024,256]{1,0:T(8,128)(2,1)S(1)} collective-permute-done((bf16[1024,256]{1,0:T(8,128)(2,1)S(1)}, bf16[1024,256]{1,0:T(8,128)(2,1)S(1)}, u32[]{:S(2)}, u32[]{:S(2)}) %collective-permute-start.66) | collective-permute-done | bytes 524320 | tf_op jit(solution)/shard_map/ppermute | solution.py:137
  522.0 10.8 %collective-permute-done.45 = bf16[1344,256]{1,0:T(8,128)(2,1)S(1)} collective-permute-done((bf16[1344,256]{1,0:T(8,128)(2,1)S(1)}, bf16[1344,256]{1,0:T(8,128)(2,1)S(1)}, u32[]{:S(2)}, u32[]{:S(2)}) %collective-permute-start.45) | collective-permute-done | bytes 688160 | tf_op jit(solution)/shard_map/ppermute | solution.py:137
  533.1 10.9 %collective-permute-done.67 = bf16[1024,256]{1,0:T(8,128)(2,1)S(1)} collective-permute-done((bf16[1024,256]{1,0:T(8,128)(2,1)S(1)}, bf16[1024,256]{1,0:T(8,128)(2,1)S(1)}, u32[]{:S(2)}, u32[]{:S(2)}) %collective-permute-start.67) | collective-permute-done | bytes 524320 | tf_op jit(solution)/shard_map/ppermute | solution.py:137
  558.1 20.7 %collective-permute-done.39 = bf16[256,2048]{1,0:T(8,128)(2,1)S(1)} collective-permute-done((bf16[256,2048]{1,0:T(8,128)(2,1)S(1)}, bf16[256,2048]{1,0:T(8,128)(2,1)S(1)}, u32[]{:S(2)}, u32[]{:S(2)}) %collective-permute-start.39) | collective-permute-done | bytes 1048608 | tf_op jit(solution)/shard_map/ppermute | solution.py:23
  (455 shorter events, 289.3 us)
Async XLA Ops:
  26.8 53.4 %collective-permute-start.1 = (bf16[256,2048]{1,0:T(8,128)(2,1)S(1)}, bf16[256,2048]{1,0:T(8,128)(2,1)}, u32[]{:S(2)}, u32[]{:S(2)}) collective-permute-start(bf16[256,2048]{1,0:T(8,128)(2,1)S(1)} %pad_maximum_fusion.refs_0_), channel_id=1, source_target_pairs={{0,2},{1,3},{2,0},{3,1},{4,6},{5,7},{6,4},{7,5},{8,10},{9,11},{10,... | collective-permute-start | bytes 3145736 | tf_op jit(solution)/shard_map/ppermute | solution.py:23
  30.1 50.1 %collective-permute-start = (bf16[256,2048]{1,0:T(8,128)(2,1)S(1)}, bf16[256,2048]{1,0:T(8,128)(2,1)S(1)}, u32[]{:S(2)}, u32[]{:S(2)}) collective-permute-start(bf16[256,2048]{1,0:T(8,128)(2,1)S(1)} %pad_maximum_fusion.refs_0_), channel_id=1, source_target_pairs={{0,1},{1,0},{2,3},{3,2},{4,5},{5,4},{6,7},{7,6},{8,9},{9,8},{10,11... | collective-permute-start | bytes 3145736 | tf_op jit(solution)/shard_map/ppermute | solution.py:23
  64.9 37.6 %collective-permute-start.35 = (bf16[256,2048]{1,0:T(8,128)(2,1)S(1)}, bf16[256,2048]{1,0:T(8,128)(2,1)}, u32[]{:S(2)}, u32[]{:S(2)}) collective-permute-start(bf16[256,2048]{1,0:T(8,128)(2,1)S(1)} %pad_maximum_fusion.1.refs_0_), channel_id=1, source_target_pairs={{0,2},{1,3},{2,0},{3,1},{4,6},{5,7},{6,4},{7,5},{8,10},{9,11},{10,... | collective-permute-start | bytes 3145736 | tf_op jit(solution)/shard_map/ppermute | solution.py:23
  91.3 38.7 %collective-permute-start.10 = (bf16[1344,256]{1,0:T(8,128)(2,1)}, bf16[1344,256]{1,0:T(8,128)(2,1)}, u32[]{:S(2)}, u32[]{:S(2)}) collective-permute-start(bf16[1344,256]{1,0:T(8,128)(2,1)} %collective-permute-done.9.refs_2_), channel_id=1, source_target_pairs={{0,8},{4,12},{8,16},{12,20},{16,24},{20,28},{24,0},{28,4},{1,9},{5... | collective-permute-start | bytes 2064392 | tf_op jit(solution)/shard_map/ppermute | solution.py:111
  138.5 69.2 %collective-permute-start.20 = (bf16[1024,256]{1,0:T(8,128)(2,1)S(1)}, bf16[1024,256]{1,0:T(8,128)(2,1)}, u32[]{:S(2)}, u32[]{:S(2)}) collective-permute-start(bf16[1024,256]{1,0:T(8,128)(2,1)S(1)} %add_add_fusion.refs_3_.refs_0_), channel_id=1, source_target_pairs={{0,4},{4,0},{8,12},{12,8},{16,20},{20,16},{24,28},{28,24},{1,5},{5... | collective-permute-start | bytes 1572872 | tf_op jit(solution)/shard_map/ppermute | solution.py:23
  140.0 69.8 %collective-permute-start.21 = (bf16[1024,256]{1,0:T(8,128)(2,1)}, bf16[1024,256]{1,0:T(8,128)(2,1)}, u32[]{:S(2)}, u32[]{:S(2)}) collective-permute-start(bf16[1024,256]{1,0:T(8,128)(2,1)} %copy-done.22), channel_id=1, source_target_pairs={{0,4},{4,0},{8,12},{12,8},{16,20},{20,16},{24,28},{28,24},{1,5},{5... | collective-permute-start | bytes 1572872 | tf_op jit(solution)/shard_map/ppermute | solution.py:23
  152.7 55.4 %collective-permute-start.26 = (bf16[1024,256]{1,0:T(8,128)(2,1)}, bf16[1024,256]{1,0:T(8,128)(2,1)}, u32[]{:S(2)}, u32[]{:S(2)}) collective-permute-start(bf16[1024,256]{1,0:T(8,128)(2,1)} %collective-permute-done.25.refs_2_.refs_8_), channel_id=1, source_target_pairs={{0,8},{4,12},{8,16},{12,20},{16,24},{20,28},{24,0},{28,4},{1,9},{5... | collective-permute-start | bytes 1572872 | tf_op jit(solution)/shard_map/ppermute | solution.py:111
  153.1 57.0 %collective-permute-start.22 = (bf16[1024,256]{1,0:T(8,128)(2,1)}, bf16[1024,256]{1,0:T(8,128)(2,1)}, u32[]{:S(2)}, u32[]{:S(2)}) collective-permute-start(bf16[1024,256]{1,0:T(8,128)(2,1)} %collective-permute-done.18.refs_5_.refs_2_), channel_id=1, source_target_pairs={{0,4},{4,0},{8,12},{12,8},{16,20},{20,16},{24,28},{28,24},{1,5},{5... | collective-permute-start | bytes 1572872 | tf_op jit(solution)/shard_map/ppermute | solution.py:23
  161.4 50.5 %collective-permute-start.23 = (bf16[1024,256]{1,0:T(8,128)(2,1)S(1)}, bf16[1024,256]{1,0:T(8,128)(2,1)}, u32[]{:S(2)}, u32[]{:S(2)}) collective-permute-start(bf16[1024,256]{1,0:T(8,128)(2,1)S(1)} %collective-permute-done.19.refs_6_.refs_3_), channel_id=1, source_target_pairs={{0,4},{4,0},{8,12},{12,8},{16,20},{20,16},{24,28},{28,24},{1,5},{5... | collective-permute-start | bytes 1572872 | tf_op jit(solution)/shard_map/ppermute | solution.py:23
  207.7 38.3 %collective-permute-start.27 = (bf16[1024,256]{1,0:T(8,128)(2,1)}, bf16[1024,256]{1,0:T(8,128)(2,1)}, u32[]{:S(2)}, u32[]{:S(2)}) collective-permute-start(bf16[1024,256]{1,0:T(8,128)(2,1)} %refs_6_.1), channel_id=1, source_target_pairs={{0,4},{4,0},{8,12},{12,8},{16,20},{20,16},{24,28},{28,24},{1,5},{5... | collective-permute-start | bytes 1572872 | tf_op jit(solution)/shard_map/ppermute | solution.py:23
  208.1 37.9 %collective-permute-start.28 = (bf16[1024,256]{1,0:T(8,128)(2,1)}, bf16[1024,256]{1,0:T(8,128)(2,1)}, u32[]{:S(2)}, u32[]{:S(2)}) collective-permute-start(bf16[1024,256]{1,0:T(8,128)(2,1)} %collective-permute-done.24.refs_1_.refs_7_), channel_id=1, source_target_pairs={{0,4},{4,0},{8,12},{12,8},{16,20},{20,16},{24,28},{28,24},{1,5},{5... | collective-permute-start | bytes 1572872 | tf_op jit(solution)/shard_map/ppermute | solution.py:23
  209.8 36.2 %collective-permute-start.29 = (bf16[1024,256]{1,0:T(8,128)(2,1)}, bf16[1024,256]{1,0:T(8,128)(2,1)}, u32[]{:S(2)}, u32[]{:S(2)}) collective-permute-start(bf16[1024,256]{1,0:T(8,128)(2,1)} %collective-permute-done.25.refs_2_.refs_8_), channel_id=1, source_target_pairs={{0,4},{4,0},{8,12},{12,8},{16,20},{20,16},{24,28},{28,24},{1,5},{5... | collective-permute-start | bytes 1572872 | tf_op jit(solution)/shard_map/ppermute | solution.py:23
  210.1 46.0 %collective-permute-start.30 = (bf16[1024,256]{1,0:T(8,128)(2,1)}, bf16[1024,256]{1,0:T(8,128)(2,1)}, u32[]{:S(2)}, u32[]{:S(2)}) collective-permute-start(bf16[1024,256]{1,0:T(8,128)(2,1)} %collective-permute-done.26.refs_3_.refs_9_), channel_id=1, source_target_pairs={{0,4},{4,0},{8,12},{12,8},{16,20},{20,16},{24,28},{28,24},{1,5},{5... | collective-permute-start | bytes 1572872 | tf_op jit(solution)/shard_map/ppermute | solution.py:23
  362.9 66.6 %collective-permute-start.64 = (bf16[1024,256]{1,0:T(8,128)(2,1)}, bf16[1024,256]{1,0:T(8,128)(2,1)}, u32[]{:S(2)}, u32[]{:S(2)}) collective-permute-start(bf16[1024,256]{1,0:T(8,128)(2,1)} %get-tuple-element.148), channel_id=1, source_target_pairs={{0,4},{4,0},{8,12},{12,8},{16,20},{20,16},{24,28},{28,24},{1,5},{5... | collective-permute-start | bytes 1572872 | tf_op jit(solution)/shard_map/ppermute | solution.py:23
  363.6 85.5 %collective-permute-start.63 = (bf16[1024,256]{1,0:T(8,128)(2,1)}, bf16[1024,256]{1,0:T(8,128)(2,1)}, u32[]{:S(2)}, u32[]{:S(2)}) collective-permute-start(bf16[1024,256]{1,0:T(8,128)(2,1)} %get-tuple-element.149), channel_id=1, source_target_pairs={{0,4},{4,0},{8,12},{12,8},{16,20},{20,16},{24,28},{28,24},{1,5},{5... | collective-permute-start | bytes 1572872 | tf_op jit(solution)/shard_map/ppermute | solution.py:23
  368.8 64.1 %collective-permute-start.50 = (bf16[1024,256]{1,0:T(8,128)(2,1)}, bf16[1024,256]{1,0:T(8,128)(2,1)}, u32[]{:S(2)}, u32[]{:S(2)}) collective-permute-start(bf16[1024,256]{1,0:T(8,128)(2,1)} %get-tuple-element.152), channel_id=1, source_target_pairs={{0,4},{4,0},{8,12},{12,8},{16,20},{20,16},{24,28},{28,24},{1,5},{5... | collective-permute-start | bytes 1572872 | tf_op jit(solution)/shard_map/ppermute | solution.py:23
  369.5 90.9 %collective-permute-start.49 = (bf16[1024,256]{1,0:T(8,128)(2,1)}, bf16[1024,256]{1,0:T(8,128)(2,1)}, u32[]{:S(2)}, u32[]{:S(2)}) collective-permute-start(bf16[1024,256]{1,0:T(8,128)(2,1)} %get-tuple-element.153), channel_id=1, source_target_pairs={{0,4},{4,0},{8,12},{12,8},{16,20},{20,16},{24,28},{28,24},{1,5},{5... | collective-permute-start | bytes 1572872 | tf_op jit(solution)/shard_map/ppermute | solution.py:23
  429.4 39.9 %collective-permute-start.32 = (bf16[256,2048]{1,0:T(8,128)(2,1)}, bf16[256,2048]{1,0:T(8,128)(2,1)}, u32[]{:S(2)}, u32[]{:S(2)}) collective-permute-start(bf16[256,2048]{1,0:T(8,128)(2,1)} %get-tuple-element.142), channel_id=1, source_target_pairs={{0,1},{1,0},{2,3},{3,2},{4,5},{5,4},{6,7},{7,6},{8,9},{9,8},{10,11... | collective-permute-start | bytes 3145736 | tf_op jit(solution)/shard_map/ppermute | solution.py:23
  449.2 42.4 %collective-permute-start.62 = (bf16[1024,256]{1,0:T(8,128)(2,1)}, bf16[1024,256]{1,0:T(8,128)(2,1)S(1)}, u32[]{:S(2)}, u32[]{:S(2)}) collective-permute-start(bf16[1024,256]{1,0:T(8,128)(2,1)} %get-tuple-element.150), channel_id=1, source_target_pairs={{0,4},{4,0},{8,12},{12,8},{16,20},{20,16},{24,28},{28,24},{1,5},{5... | collective-permute-start | bytes 1572872 | tf_op jit(solution)/shard_map/ppermute | solution.py:23
  457.8 50.0 %collective-permute-start.48 = (bf16[1024,256]{1,0:T(8,128)(2,1)}, bf16[1024,256]{1,0:T(8,128)(2,1)S(1)}, u32[]{:S(2)}, u32[]{:S(2)}) collective-permute-start(bf16[1024,256]{1,0:T(8,128)(2,1)} %get-tuple-element.154), channel_id=1, source_target_pairs={{0,4},{4,0},{8,12},{12,8},{16,20},{20,16},{24,28},{28,24},{1,5},{5... | collective-permute-start | bytes 1572872 | tf_op jit(solution)/shard_map/ppermute | solution.py:23
  493.0 39.7 %collective-permute-start.45 = (bf16[1344,256]{1,0:T(8,128)(2,1)S(1)}, bf16[1344,256]{1,0:T(8,128)(2,1)S(1)}, u32[]{:S(2)}, u32[]{:S(2)}) collective-permute-start(bf16[1344,256]{1,0:T(8,128)(2,1)S(1)} %add_convert_fusion.1), channel_id=1, source_target_pairs={{0,8},{4,12},{8,16},{12,20},{16,24},{20,28},{24,0},{28,4},{1,9},{5... | collective-permute-start | bytes 2064392 | tf_op jit(solution)/shard_map/ppermute | solution.py:137
  507.8 37.3 %collective-permute-start.47 = (bf16[1024,256]{1,0:T(8,128)(2,1)S(1)}, bf16[1024,256]{1,0:T(8,128)(2,1)S(1)}, u32[]{:S(2)}, u32[]{:S(2)}) collective-permute-start(bf16[1024,256]{1,0:T(8,128)(2,1)S(1)} %copy-done.40), channel_id=1, source_target_pairs={{0,4},{4,0},{8,12},{12,8},{16,20},{20,16},{24,28},{28,24},{1,5},{5... | collective-permute-start | bytes 1572872 | tf_op jit(solution)/shard_map/ppermute | solution.py:23
  518.0 36.4 %collective-permute-start.31 = (bf16[256,2048]{1,0:T(8,128)(2,1)S(1)}, bf16[256,2048]{1,0:T(8,128)(2,1)S(1)}, u32[]{:S(2)}, u32[]{:S(2)}) collective-permute-start(bf16[256,2048]{1,0:T(8,128)(2,1)S(1)} %copy-done.29), channel_id=1, source_target_pairs={{0,1},{1,0},{2,3},{3,2},{4,5},{5,4},{6,7},{7,6},{8,9},{9,8},{10,11... | collective-permute-start | bytes 3145736 | tf_op jit(solution)/shard_map/ppermute | solution.py:23
  545.2 35.8 %collective-permute-start.40 = (bf16[1344,256]{1,0:T(8,128)(2,1)S(1)}, bf16[1344,256]{1,0:T(8,128)(2,1)S(1)}, u32[]{:S(2)}, u32[]{:S(2)}) collective-permute-start(bf16[1344,256]{1,0:T(8,128)(2,1)S(1)} %copy-done.32), channel_id=1, source_target_pairs={{0,4},{4,0},{8,12},{12,8},{16,20},{20,16},{24,28},{28,24},{1,5},{5... | collective-permute-start | bytes 2064392 | tf_op jit(solution)/shard_map/ppermute | solution.py:23
  (107 other events, 2309.3 us)

commit v2 on v1

--- a/solution.py
+++ b/solution.py
@@ -112,30 +112,43 @@
     return mine + other
 
 
-def scatter_dp(left, right):
+def scatter_dp(products):
     count = lax.axis_size(DP)
 
-    def multiply(some, kind):
+    def multiply(left, some, kind):
         return lax.dot_general(left, some, (((0,), (0,)), ((), ())), preferred_element_type=kind)
 
     if not ringed(DP):
-        return lax.psum_scatter(multiply(right, F32), DP, scatter_dimension=1, tiled=True)
+        return [
+            lax.psum_scatter(multiply(left, right, F32), DP, scatter_dimension=1, tiled=True)
+            for left, right, _ in products
+        ]
     steps = count // 2
-    half = right.shape[1] // 2
+    half = products[0][1].shape[1] // 2
     wide = half // steps
     ring = [(i, (i + 2) % count) for i in range(count)]
-    other = multiply(right[:, half:], BF16)
-    mine = multiply(right[:, :half], BF16)
+    sides = []
+    for left, right, label in products:
+        other = multiply(left, right[:, half:], BF16)
+        mine = multiply(left, right[:, :half], BF16)
+        sides.append((mine, other, label))
     carried = None
     for step in range(1, steps + 1):
         at = step % steps * wide
-        came = flip(other[:, at : at + wide], DP, 1)
-        total = mine[:, at : at + wide].astype(F32) + came.astype(F32)
+        totals = []
+        for mine, other, label in sides:
+            came = flip(other[:, at : at + wide], DP, 1)
+            totals.append(mine[:, at : at + wide].astype(F32) + came.astype(F32))
         if carried is not None:
-            total = total + carried.astype(F32)
+            place = 0
+            for i, total in enumerate(totals):
+                totals[i] = total + carried[place : place + total.shape[0]].astype(F32)
+                place += total.shape[0]
         if step < steps:
-            carried = lax.ppermute(total.astype(BF16), DP, ring)
-    return total
+            joint = [total.astype(BF16) for total in totals]
+            joint = jnp.concatenate(joint, axis=0) if len(joint) > 1 else joint[0]
+            carried = lax.ppermute(joint, DP, ring)
+    return totals
 
 
 def scatter_state(whole):
@@ -816,7 +829,6 @@
     scale_row = lax.rsqrt(square / active + EPSILON)
     out_scale = scale_row.reshape(seq_rows, 1)
     normed_out = run_normalize(mixed, gate, out_scale, gain_mask)
-    grad_out_proj = scatter_dp(normed_out, cot_all)
 
     out_grad, aligned, norm_sums = run_gate_grad(cot_all, mixed, gate, out_scale, gain_mask, mask, w_o)
     grad_norm_out = norm_sums[0]
@@ -833,7 +845,7 @@
 
     (out_whole,) = run_products(normed_out, w_o)
     block_out = (tokens + from_ring(scatter_state(out_whole), DP)).astype(BF16)
-    grad_in_gate = scatter_dp(gate_grad, normed_all)
+    grad_out_proj, grad_in_gate = scatter_dp([(normed_out, cot_all, "o"), (gate_grad, normed_all, "g")])
     x_grad, conv_sums, skip_sums, head_sums = run_scan_backward(
         x_proj, act, mixed_grad.astype(BF16), starts, scan_params
     )
@@ -841,7 +853,7 @@
     grad_d_skip = jnp.sum(skip_sums.reshape(heads, P_SIZE), axis=1)
     grad_dt_bias, grad_a_log = head_sums[0], head_sums[1]
 
-    grad_in_x = scatter_dp(x_grad, normed_all)
+    (grad_in_x,) = scatter_dp([(x_grad, normed_all, "x")])
     x_low, gate_low = grad_in_x.astype(BF16), grad_in_gate.astype(BF16)
     held = {"v": x_low[:cols], "b": x_low[cols:], "g": gate_low}
     pieces = [grad_in_x, grad_in_gate]

time: 612 us -> 647 us (1.057)
  waiting for transfers between devices: 217 us -> 253 us
    ppermute x9 -> x6, waiting for transfers between devices: 61.4 us -> 84.1 us  [scatter_dp(): carried = lax.ppermute(joint, DP, ring)]
    ppermute x41, waiting for transfers between devices: 72.1 us -> 84.7 us  [flip(): lax.ppermute(value, axis, [(i, i ^ bit) for i in range(lax.axis_size(axis...]
    unnamed x192 -> x188, local copies, waits for them, and re-layouts: 13.9 us -> 16.7 us
  transfers between devices with their start and end apart: 73 -> 70, of which waited for: 25 -> 23; matrix products, arithmetic and copies ran while one was open for 15% -> 14% of each run, Pallas kernels for 15% -> 15%
where the time goes in v2:
time: 647 us; the launch traced here: 636 us
  waiting for transfers between devices  253 us (39%)
  Pallas kernels  179 us (28%)
  starting transfers between devices  75.7 us (12%)
  local copies, waits for them, and re-layouts  46 us (7%)
  other arithmetic  39.5 us (6%)
  matrix products  27.7 us (4%)
  blocking collectives  11.9 us (2%)
    ppermute x41, waiting for transfers between devices, flip(): lax.ppermute(value, axis, [(i, i ^ bit) for i in range(lax.axis_size(axis...  84.7 us
    ppermute x6, waiting for transfers between devices, scatter_dp(): carried = lax.ppermute(joint, DP, ring)  84.1 us
    pallas_call x4, Pallas kernels, run_scan_backward(): pl.pallas_call(functools.partial(scan_backward, held is None, at == 0), g...  66.1 us
    ppermute x9, waiting for transfers between devices, gather_dp(): mine.append(lax.ppermute(mine[step], DP, ring))  64.7 us
    ppermute x41, starting transfers between devices, flip(): lax.ppermute(value, axis, [(i, i ^ bit) for i in range(lax.axis_size(axis...  48 us
    pallas_call x3, Pallas kernels, run_products(): pl.pallas_call(kernel, grid=(rows // TALL,), in_specs=[tall_spec(left)] +...  33.5 us
    dot_general x6, matrix products, multiply(): lax.dot_general(left, some, (((0,), (0,)), ((), ())), preferred_element_t...  27.7 us
    pallas_call x2, Pallas kernels, run_scan_forward(): pl.pallas_call(functools.partial(scan_forward, held is None), grid=(per,)...  21.8 us
  transfers between devices with their start and end apart: 70, of which 23 were waited for; matrix products, arithmetic and copies ran while one was open for 14% of the time, Pallas kernels for 15%

profile of v2, /device:TPU:0, one launch (start us, length us, event | category | flops | bytes accessed | tf_op | source)
XLA Modules:
  0.0 635.6 jit_solution(6129555845922565661)
XLA Ops:
  51.5 13.3 %collective-permute-done.16 = bf16[1024,256]{1,0:T(8,128)(2,1)S(1)} collective-permute-done((bf16[1024,256]{1,0:T(8,128)(2,1)S(1)}, bf16[1024,256]{1,0:T(8,128)(2,1)S(1)}, u32[]{:S(2)}, u32[]{:S(2)}) %collective-permute-start.16) | collective-permute-done | bytes 524320 | tf_op jit(solution)/shard_map/ppermute | solution.py:792
  81.3 9.9 %collective-permute-done.9.refs_2_ = bf16[1344,256]{1,0:T(8,128)(2,1)} collective-permute-done((bf16[1344,256]{1,0:T(8,128)(2,1)S(1)}, bf16[1344,256]{1,0:T(8,128)(2,1)}, u32[]{:S(2)}, u32[]{:S(2)}) %collective-permute-start.9) | collective-permute-done | bytes 688160 | tf_op jit(solution)/shard_map/ppermute | solution.py:111
  91.2 11.1 %collective-permute-done.17.refs_4_.refs_1_ = bf16[1024,256]{1,0:T(8,128)(2,1)S(1)} collective-permute-done((bf16[1024,256]{1,0:T(8,128)(2,1)S(1)}, bf16[1024,256]{1,0:T(8,128)(2,1)S(1)}, u32[]{:S(2)}, u32[]{:S(2)}) %collective-permute-start.17) | collective-permute-done | bytes 524320 | tf_op jit(solution)/shard_map/ppermute | solution.py:111
  108.7 19.7 %collective-permute-done.18.refs_5_.refs_2_ = bf16[1024,256]{1,0:T(8,128)(2,1)} collective-permute-done((bf16[1024,256]{1,0:T(8,128)(2,1)S(1)}, bf16[1024,256]{1,0:T(8,128)(2,1)}, u32[]{:S(2)}, u32[]{:S(2)}) %collective-permute-start.18) | collective-permute-done | bytes 524320 | tf_op jit(solution)/shard_map/ppermute | solution.py:111
  140.5 12.1 %collective-permute-done.19.refs_6_.refs_3_ = bf16[1024,256]{1,0:T(8,128)(2,1)S(1)} collective-permute-done((bf16[1024,256]{1,0:T(8,128)(2,1)}, bf16[1024,256]{1,0:T(8,128)(2,1)S(1)}, u32[]{:S(2)}, u32[]{:S(2)}) %collective-permute-start.19) | collective-permute-done | bytes 524320 | tf_op jit(solution)/shard_map/ppermute | solution.py:111
  173.8 12.0 %pj.1.refs_0_.refs_1_ = bf16[1024,1344]{1,0:T(8,128)(2,1)} custom-call(bf16[1024,2048]{1,0:T(8,128)(2,1)} %shard_map.221.left_ref.refs_0_.refs_9_, bf16[1344,256]{1,0:T(8,128)(2,1)} %copy-done.11, bf16[1344,256]{1,0:T(8,128)(2,1)} %copy-done.18, bf16[1344,256]{1,0:T(8,128)(2,1)} %collective-permute-done.9.refs_2_, ...), custom_call_target="tpu_custom_call" | custom-call | tf_op jit(solution)/shard_map/pj/pallas_call | solution.py:516
  185.8 10.8 %shard_map.222 = (bf16[1024,1280]{1,0:T(8,128)(2,1)}, f32[1024,1024]{1,0:T(8,128)}, f32[4096,128]{1,0:T(8,128)}, f32[8,1280]{1,0:T(8,128)}, f32[1024,128]{1,0:T(8,128)}) custom-call(bf16[1024,1344]{1,0:T(8,128)(2,1)} %pj.1.refs_0_.refs_1_, f32[4,1280]{1,0:T(4,128)} %pad_maximum_fusion.5.refs_1_.refs_5_, f32[1,1280]{1,0:T(1,128)} %broadcast_in_dim.40.refs_2_.refs_6_, ...), custom_call_target="tpu_custom_call" | custom-call | tf_op jit(solution)/shard_map/pallas_call | solution.py:549
  196.6 11.0 %shard_map.223 = (bf16[1024,1280]{1,0:T(8,128)(2,1)}, f32[1024,1024]{1,0:T(8,128)}, f32[4096,128]{1,0:T(8,128)}, f32[8,1280]{1,0:T(8,128)}, f32[1024,128]{1,0:T(8,128)}) custom-call(bf16[1024,1344]{1,0:T(8,128)(2,1)} %pj.1.refs_0_.refs_1_, ...), custom_call_target="tpu_custom_call", output_to_operand_aliasing={{0}: (9, {}), {1}: (10, {}), {2}: (11, {}), {3}: (12, {}), ... | custom-call | tf_op jit(solution)/shard_map/pallas_call | solution.py:549
  211.7 11.0 %gf.1 = (bf16[1024,1024]{1,0:T(8,128)(2,1)}, f32[8,1024]{1,0:T(8,128)}) custom-call(bf16[1024,2048]{1,0:T(8,128)(2,1)} %shard_map.221.left_ref.refs_0_.refs_9_, f32[1024,1024]{1,0:T(8,128)} %get-tuple-element.103.refs_1_.mixed_ref, f32[1,1024]{1,0:T(1,128)} %compare_convert_fusion.refs_2_.refs_5_, bf16[1024,256]{1,0:T(8,128)(2,1)} %copy-done.12, ...), custom_call_target="tpu_custom_call" | custom-call | tf_op jit(solution)/shard_map/gf/pallas_call | solution.py:589
  245.9 10.0 %collective-permute-done.30.refs_7_.refs_13_ = bf16[1024,256]{1,0:T(8,128)(2,1)} collective-permute-done((bf16[1024,256]{1,0:T(8,128)(2,1)}, bf16[1024,256]{1,0:T(8,128)(2,1)}, u32[]{:S(2)}, u32[]{:S(2)}) %collective-permute-start.30) | collective-permute-done | bytes 524320 | tf_op jit(solution)/shard_map/ppermute | solution.py:23
  256.0 12.6 %gb.1 = (f32[1024,1024]{1,0:T(8,128)}, f32[8,1024]{1,0:T(8,128)}, f32[1,1024]{1,0:T(1,128)}) custom-call(bf16[1024,2048]{1,0:T(8,128)(2,1)} %shard_map.225.refs_0_, f32[1024,1024]{1,0:T(8,128)} %get-tuple-element.103.refs_1_.mixed_ref, bf16[1024,1024]{1,0:T(8,128)(2,1)} %get-tuple-element.104.gate_ref.refs_2_, f32[1024,1]{1,0:T(8,128)} %copy.64.scale_ref.refs_3_, ...), custom_call_target="tpu_custom_call" | custom-call | tf_op jit(solution)/shard_map/gb/pallas_call | solution.py:636
  282.1 16.2 %shard_map.226 = (bf16[1024,1344]{1,0:T(8,128)(2,1)}, f32[8,1280]{1,0:T(8,128)}, f32[1024,128]{1,0:T(8,128)}, f32[8,1280]{1,0:T(8,128)}, f32[1,1024]{1,0:T(1,128)}, /*index=5*/f32[8,16]{1,0:T(8,128)}) custom-call(bf16[1024,1344]{1,0:T(8,128)(2,1)} %pj.1.refs_0_.refs_1_, bf16[1024,1344]{1,0:T(8,128)(2,1)} %pj.1.refs_0_.refs_1_, ...), custom_call_target="tpu_custom_call" | custom-call | tf_op jit(solution)/shard_map/pallas_call | solution.py:720
  298.3 16.6 %shard_map.227 = (bf16[1024,1344]{1,0:T(8,128)(2,1)}, f32[8,1280]{1,0:T(8,128)}, f32[1024,128]{1,0:T(8,128)}, f32[8,1280]{1,0:T(8,128)}, f32[1,1024]{1,0:T(1,128)}, /*index=5*/f32[8,16]{1,0:T(8,128)}) custom-call(bf16[1024,1344]{1,0:T(8,128)(2,1)} %pj.1.refs_0_.refs_1_, ...), custom_call_target="tpu_custom_call", output_to_operand_aliasing={{0}: (13, {}), {1}: (14, {}), {2}: (15, {}), {3}: (16, {}),... | custom-call | tf_op jit(solution)/shard_map/pallas_call | solution.py:720
  314.9 16.8 %shard_map.228 = (bf16[1024,1344]{1,0:T(8,128)(2,1)}, f32[8,1280]{1,0:T(8,128)}, f32[1024,128]{1,0:T(8,128)}, f32[8,1280]{1,0:T(8,128)}, f32[1,1024]{1,0:T(1,128)}, /*index=5*/f32[8,16]{1,0:T(8,128)}) custom-call(bf16[1024,1344]{1,0:T(8,128)(2,1)} %pj.1.refs_0_.refs_1_, ...), custom_call_target="tpu_custom_call", output_to_operand_aliasing={{0}: (13, {}), {1}: (14, {}), {2}: (15, {}), {3}: (16, {}),... | custom-call | tf_op jit(solution)/shard_map/pallas_call | solution.py:720
  331.7 16.5 %shard_map.229 = (bf16[1024,1344]{1,0:T(8,128)(2,1)}, f32[8,1280]{1,0:T(8,128)}, f32[1024,128]{1,0:T(8,128)}, f32[8,1280]{1,0:T(8,128)}, f32[1,1024]{1,0:T(1,128)}, /*index=5*/f32[8,16]{1,0:T(8,128)}) custom-call(bf16[1024,1344]{1,0:T(8,128)(2,1)} %pj.1.refs_0_.refs_1_, ...), custom_call_target="tpu_custom_call", output_to_operand_aliasing={{0}: (13, {}), {1}: (14, {}), {2}: (15, {}), {3}: (16, {}),... | custom-call | tf_op jit(solution)/shard_map/pallas_call | solution.py:720
  370.3 12.3 %shard_map.230.refs_8_ = bf16[1024,2048]{1,0:T(8,128)(2,1)} custom-call(bf16[1024,1344]{1,0:T(8,128)(2,1)} %get-tuple-element.126.left_ref, bf16[1344,256]{1,0:T(8,128)(2,1)} %copy-done.11, bf16[1344,256]{1,0:T(8,128)(2,1)} %copy-done.18, bf16[1344,256]{1,0:T(8,128)(2,1)} %collective-permute-done.9.refs_2_, ...), custom_call_target="tpu_custom_call" | custom-call | tf_op jit(solution)/shard_map/pallas_call | solution.py:681
  382.7 11.9 %shard_map.231 = (bf16[1024,2048]{1,0:T(8,128)(2,1)}, f32[1,2048]{1,0:T(1,128)}) custom-call(bf16[1024,1024]{1,0:T(8,128)(2,1)} %get-tuple-element.138.left_ref, bf16[1024,256]{1,0:T(8,128)(2,1)} %copy-done.12, bf16[1024,256]{1,0:T(8,128)(2,1)} %copy-done.21, bf16[1024,256]{1,0:T(8,128)(2,1)} %collective-permute-done.18.refs_5_.refs_2_, ...), custom_call_target="tpu_custom_call" | custom-call | tf_op jit(solution)/shard_map/pallas_call | solution.py:681
  422.5 20.0 %collective-permute-done.67 = f32[224,128]{1,0:T(8,128)S(1)} collective-permute-done((f32[224,128]{1,0:T(8,128)S(1)}, f32[224,128]{1,0:T(8,128)S(1)}, u32[]{:S(2)}, u32[]{:S(2)}) %collective-permute-start.67) | collective-permute-done | bytes 114720 | tf_op jit(solution)/shard_map/ppermute | solution.py:23
  470.8 9.8 %collective-permute-done.42 = bf16[1344,256]{1,0:T(8,128)(2,1)} collective-permute-done((bf16[1344,256]{1,0:T(8,128)(2,1)}, bf16[1344,256]{1,0:T(8,128)(2,1)}, u32[]{:S(2)}, u32[]{:S(2)}) %collective-permute-start.42) | collective-permute-done | bytes 688160 | tf_op jit(solution)/shard_map/ppermute | solution.py:23
  488.9 25.3 %collective-permute-done.52 = bf16[2048,256]{1,0:T(8,128)(2,1)S(1)} collective-permute-done((bf16[2048,256]{1,0:T(8,128)(2,1)}, bf16[2048,256]{1,0:T(8,128)(2,1)S(1)}, u32[]{:S(2)}, u32[]{:S(2)}) %collective-permute-start.52) | collective-permute-done | bytes 1048608 | tf_op jit(solution)/shard_map/ppermute | solution.py:150
  527.4 10.1 %collective-permute-done.33 = bf16[256,2048]{1,0:T(8,128)(2,1)S(1)} collective-permute-done((bf16[256,2048]{1,0:T(8,128)(2,1)S(1)}, bf16[256,2048]{1,0:T(8,128)(2,1)S(1)}, u32[]{:S(2)}, u32[]{:S(2)}) %collective-permute-start.33) | collective-permute-done | bytes 1048608 | tf_op jit(solution)/shard_map/ppermute | solution.py:23
  542.2 14.3 %collective-permute-done.39 = bf16[256,2048]{1,0:T(8,128)(2,1)S(1)} collective-permute-done((bf16[256,2048]{1,0:T(8,128)(2,1)S(1)}, bf16[256,2048]{1,0:T(8,128)(2,1)S(1)}, u32[]{:S(2)}, u32[]{:S(2)}) %collective-permute-start.39) | collective-permute-done | bytes 1048608 | tf_op jit(solution)/shard_map/ppermute | solution.py:23
  559.8 24.6 %collective-permute-done.54 = bf16[2048,256]{1,0:T(8,128)(2,1)S(1)} collective-permute-done((bf16[2048,256]{1,0:T(8,128)(2,1)S(1)}, bf16[2048,256]{1,0:T(8,128)(2,1)S(1)}, u32[]{:S(2)}, u32[]{:S(2)}) %collective-permute-start.54) | collective-permute-done | bytes 1048608 | tf_op jit(solution)/shard_map/ppermute | solution.py:150
  585.5 13.7 %collective-permute-done.46 = bf16[1344,256]{1,0:T(8,128)(2,1)S(1)} collective-permute-done((bf16[1344,256]{1,0:T(8,128)(2,1)S(1)}, bf16[1344,256]{1,0:T(8,128)(2,1)S(1)}, u32[]{:S(2)}, u32[]{:S(2)}) %collective-permute-start.46) | collective-permute-done | bytes 688160 | tf_op jit(solution)/shard_map/ppermute | solution.py:150
  (445 shorter events, 290.7 us)
Async XLA Ops:
  26.7 53.4 %collective-permute-start.1 = (bf16[256,2048]{1,0:T(8,128)(2,1)S(1)}, bf16[256,2048]{1,0:T(8,128)(2,1)}, u32[]{:S(2)}, u32[]{:S(2)}) collective-permute-start(bf16[256,2048]{1,0:T(8,128)(2,1)S(1)} %pad_maximum_fusion.refs_0_), channel_id=1, source_target_pairs={{0,2},{1,3},{2,0},{3,1},{4,6},{5,7},{6,4},{7,5},{8,10},{9,11},{10,... | collective-permute-start | bytes 3145736 | tf_op jit(solution)/shard_map/ppermute | solution.py:23
  30.0 50.1 %collective-permute-start = (bf16[256,2048]{1,0:T(8,128)(2,1)S(1)}, bf16[256,2048]{1,0:T(8,128)(2,1)S(1)}, u32[]{:S(2)}, u32[]{:S(2)}) collective-permute-start(bf16[256,2048]{1,0:T(8,128)(2,1)S(1)} %pad_maximum_fusion.refs_0_), channel_id=1, source_target_pairs={{0,1},{1,0},{2,3},{3,2},{4,5},{5,4},{6,7},{7,6},{8,9},{9,8},{10,11... | collective-permute-start | bytes 3145736 | tf_op jit(solution)/shard_map/ppermute | solution.py:23
  64.8 37.6 %collective-permute-start.35 = (bf16[256,2048]{1,0:T(8,128)(2,1)S(1)}, bf16[256,2048]{1,0:T(8,128)(2,1)}, u32[]{:S(2)}, u32[]{:S(2)}) collective-permute-start(bf16[256,2048]{1,0:T(8,128)(2,1)S(1)} %pad_maximum_fusion.1.refs_0_), channel_id=1, source_target_pairs={{0,2},{1,3},{2,0},{3,1},{4,6},{5,7},{6,4},{7,5},{8,10},{9,11},{10,... | collective-permute-start | bytes 3145736 | tf_op jit(solution)/shard_map/ppermute | solution.py:23
  91.2 38.7 %collective-permute-start.10 = (bf16[1344,256]{1,0:T(8,128)(2,1)}, bf16[1344,256]{1,0:T(8,128)(2,1)}, u32[]{:S(2)}, u32[]{:S(2)}) collective-permute-start(bf16[1344,256]{1,0:T(8,128)(2,1)} %collective-permute-done.9.refs_2_), channel_id=1, source_target_pairs={{0,8},{4,12},{8,16},{12,20},{16,24},{20,28},{24,0},{28,4},{1,9},{5... | collective-permute-start | bytes 2064392 | tf_op jit(solution)/shard_map/ppermute | solution.py:111
  138.5 69.1 %collective-permute-start.20 = (bf16[1024,256]{1,0:T(8,128)(2,1)S(1)}, bf16[1024,256]{1,0:T(8,128)(2,1)}, u32[]{:S(2)}, u32[]{:S(2)}) collective-permute-start(bf16[1024,256]{1,0:T(8,128)(2,1)S(1)} %add_add_fusion.refs_3_.refs_0_), channel_id=1, source_target_pairs={{0,4},{4,0},{8,12},{12,8},{16,20},{20,16},{24,28},{28,24},{1,5},{5... | collective-permute-start | bytes 1572872 | tf_op jit(solution)/shard_map/ppermute | solution.py:23
  140.0 69.7 %collective-permute-start.21 = (bf16[1024,256]{1,0:T(8,128)(2,1)}, bf16[1024,256]{1,0:T(8,128)(2,1)}, u32[]{:S(2)}, u32[]{:S(2)}) collective-permute-start(bf16[1024,256]{1,0:T(8,128)(2,1)} %copy-done.21), channel_id=1, source_target_pairs={{0,4},{4,0},{8,12},{12,8},{16,20},{20,16},{24,28},{28,24},{1,5},{5... | collective-permute-start | bytes 1572872 | tf_op jit(solution)/shard_map/ppermute | solution.py:23
  152.6 55.4 %collective-permute-start.26 = (bf16[1024,256]{1,0:T(8,128)(2,1)}, bf16[1024,256]{1,0:T(8,128)(2,1)}, u32[]{:S(2)}, u32[]{:S(2)}) collective-permute-start(bf16[1024,256]{1,0:T(8,128)(2,1)} %collective-permute-done.25.refs_2_.refs_8_), channel_id=1, source_target_pairs={{0,8},{4,12},{8,16},{12,20},{16,24},{20,28},{24,0},{28,4},{1,9},{5... | collective-permute-start | bytes 1572872 | tf_op jit(solution)/shard_map/ppermute | solution.py:111
  153.1 56.9 %collective-permute-start.22 = (bf16[1024,256]{1,0:T(8,128)(2,1)}, bf16[1024,256]{1,0:T(8,128)(2,1)}, u32[]{:S(2)}, u32[]{:S(2)}) collective-permute-start(bf16[1024,256]{1,0:T(8,128)(2,1)} %collective-permute-done.18.refs_5_.refs_2_), channel_id=1, source_target_pairs={{0,4},{4,0},{8,12},{12,8},{16,20},{20,16},{24,28},{28,24},{1,5},{5... | collective-permute-start | bytes 1572872 | tf_op jit(solution)/shard_map/ppermute | solution.py:23
  161.3 50.4 %collective-permute-start.23 = (bf16[1024,256]{1,0:T(8,128)(2,1)S(1)}, bf16[1024,256]{1,0:T(8,128)(2,1)}, u32[]{:S(2)}, u32[]{:S(2)}) collective-permute-start(bf16[1024,256]{1,0:T(8,128)(2,1)S(1)} %collective-permute-done.19.refs_6_.refs_3_), channel_id=1, source_target_pairs={{0,4},{4,0},{8,12},{12,8},{16,20},{20,16},{24,28},{28,24},{1,5},{5... | collective-permute-start | bytes 1572872 | tf_op jit(solution)/shard_map/ppermute | solution.py:23
  207.6 38.3 %collective-permute-start.27 = (bf16[1024,256]{1,0:T(8,128)(2,1)}, bf16[1024,256]{1,0:T(8,128)(2,1)}, u32[]{:S(2)}, u32[]{:S(2)}) collective-permute-start(bf16[1024,256]{1,0:T(8,128)(2,1)} %refs_6_.1), channel_id=1, source_target_pairs={{0,4},{4,0},{8,12},{12,8},{16,20},{20,16},{24,28},{28,24},{1,5},{5... | collective-permute-start | bytes 1572872 | tf_op jit(solution)/shard_map/ppermute | solution.py:23
  208.0 37.9 %collective-permute-start.28 = (bf16[1024,256]{1,0:T(8,128)(2,1)}, bf16[1024,256]{1,0:T(8,128)(2,1)}, u32[]{:S(2)}, u32[]{:S(2)}) collective-permute-start(bf16[1024,256]{1,0:T(8,128)(2,1)} %collective-permute-done.24.refs_1_.refs_7_), channel_id=1, source_target_pairs={{0,4},{4,0},{8,12},{12,8},{16,20},{20,16},{24,28},{28,24},{1,5},{5... | collective-permute-start | bytes 1572872 | tf_op jit(solution)/shard_map/ppermute | solution.py:23
  209.7 36.2 %collective-permute-start.29 = (bf16[1024,256]{1,0:T(8,128)(2,1)}, bf16[1024,256]{1,0:T(8,128)(2,1)}, u32[]{:S(2)}, u32[]{:S(2)}) collective-permute-start(bf16[1024,256]{1,0:T(8,128)(2,1)} %collective-permute-done.25.refs_2_.refs_8_), channel_id=1, source_target_pairs={{0,4},{4,0},{8,12},{12,8},{16,20},{20,16},{24,28},{28,24},{1,5},{5... | collective-permute-start | bytes 1572872 | tf_op jit(solution)/shard_map/ppermute | solution.py:23
  210.0 46.0 %collective-permute-start.30 = (bf16[1024,256]{1,0:T(8,128)(2,1)}, bf16[1024,256]{1,0:T(8,128)(2,1)}, u32[]{:S(2)}, u32[]{:S(2)}) collective-permute-start(bf16[1024,256]{1,0:T(8,128)(2,1)} %collective-permute-done.26.refs_3_.refs_9_), channel_id=1, source_target_pairs={{0,4},{4,0},{8,12},{12,8},{16,20},{20,16},{24,28},{28,24},{1,5},{5... | collective-permute-start | bytes 1572872 | tf_op jit(solution)/shard_map/ppermute | solution.py:23
  362.8 84.8 %collective-permute-start.50 = (bf16[1024,256]{1,0:T(8,128)(2,1)}, bf16[1024,256]{1,0:T(8,128)(2,1)}, u32[]{:S(2)}, u32[]{:S(2)}) collective-permute-start(bf16[1024,256]{1,0:T(8,128)(2,1)} %get-tuple-element.148), channel_id=1, source_target_pairs={{0,4},{4,0},{8,12},{12,8},{16,20},{20,16},{24,28},{28,24},{1,5},{5... | collective-permute-start | bytes 1572872 | tf_op jit(solution)/shard_map/ppermute | solution.py:23
  402.7 85.4 %collective-permute-start.49 = (bf16[1024,256]{1,0:T(8,128)(2,1)}, bf16[1024,256]{1,0:T(8,128)(2,1)}, u32[]{:S(2)}, u32[]{:S(2)}) collective-permute-start(bf16[1024,256]{1,0:T(8,128)(2,1)} %get-tuple-element.149), channel_id=1, source_target_pairs={{0,4},{4,0},{8,12},{12,8},{16,20},{20,16},{24,28},{28,24},{1,5},{5... | collective-permute-start | bytes 1572872 | tf_op jit(solution)/shard_map/ppermute | solution.py:23
  406.7 82.2 %collective-permute-start.53 = (bf16[1024,256]{1,0:T(8,128)(2,1)}, bf16[1024,256]{1,0:T(8,128)(2,1)}, u32[]{:S(2)}, u32[]{:S(2)}) collective-permute-start(bf16[1024,256]{1,0:T(8,128)(2,1)} %get-tuple-element.153), channel_id=1, source_target_pairs={{0,4},{4,0},{8,12},{12,8},{16,20},{20,16},{24,28},{28,24},{1,5},{5... | collective-permute-start | bytes 1572872 | tf_op jit(solution)/shard_map/ppermute | solution.py:23
  407.8 41.8 %collective-permute-start.51 = (bf16[1024,256]{1,0:T(8,128)(2,1)}, bf16[1024,256]{1,0:T(8,128)(2,1)}, u32[]{:S(2)}, u32[]{:S(2)}) collective-permute-start(bf16[1024,256]{1,0:T(8,128)(2,1)} %get-tuple-element.154), channel_id=1, source_target_pairs={{0,4},{4,0},{8,12},{12,8},{16,20},{20,16},{24,28},{28,24},{1,5},{5... | collective-permute-start | bytes 1572872 | tf_op jit(solution)/shard_map/ppermute | solution.py:23
  480.5 36.4 %collective-permute-start.41 = (bf16[1344,256]{1,0:T(8,128)(2,1)}, bf16[1344,256]{1,0:T(8,128)(2,1)S(1)}, u32[]{:S(2)}, u32[]{:S(2)}) collective-permute-start(bf16[1344,256]{1,0:T(8,128)(2,1)} %get-tuple-element.146), channel_id=1, source_target_pairs={{0,4},{4,0},{8,12},{12,8},{16,20},{20,16},{24,28},{28,24},{1,5},{5... | collective-permute-start | bytes 2064392 | tf_op jit(solution)/shard_map/ppermute | solution.py:23
  487.6 38.7 %collective-permute-start.45 = (bf16[1344,256]{1,0:T(8,128)(2,1)S(1)}, bf16[1344,256]{1,0:T(8,128)(2,1)S(1)}, u32[]{:S(2)}, u32[]{:S(2)}) collective-permute-start(bf16[1344,256]{1,0:T(8,128)(2,1)S(1)} %add_convert_fusion.1), channel_id=1, source_target_pairs={{0,8},{4,12},{8,16},{12,20},{16,24},{20,28},{24,0},{28,4},{1,9},{5... | collective-permute-start | bytes 2064392 | tf_op jit(solution)/shard_map/ppermute | solution.py:150
  488.1 114.0 %collective-permute-start.64 = (bf16[1024,256]{1,0:T(8,128)(2,1)}, bf16[1024,256]{1,0:T(8,128)(2,1)S(1)}, u32[]{:S(2)}, u32[]{:S(2)}) collective-permute-start(bf16[1024,256]{1,0:T(8,128)(2,1)} %get-tuple-element.147), channel_id=1, source_target_pairs={{0,4},{4,0},{8,12},{12,8},{16,20},{20,16},{24,28},{28,24},{1,5},{5... | collective-permute-start | bytes 1572872 | tf_op jit(solution)/shard_map/ppermute | solution.py:23
  488.9 38.4 %collective-permute-start.31 = (bf16[256,2048]{1,0:T(8,128)(2,1)S(1)}, bf16[256,2048]{1,0:T(8,128)(2,1)S(1)}, u32[]{:S(2)}, u32[]{:S(2)}) collective-permute-start(bf16[256,2048]{1,0:T(8,128)(2,1)S(1)} %copy-done.29), channel_id=1, source_target_pairs={{0,1},{1,0},{2,3},{3,2},{4,5},{5,4},{6,7},{7,6},{8,9},{9,8},{10,11... | collective-permute-start | bytes 3145736 | tf_op jit(solution)/shard_map/ppermute | solution.py:23
  517.9 40.4 %collective-permute-start.48 = (bf16[1024,256]{1,0:T(8,128)(2,1)S(1)}, bf16[1024,256]{1,0:T(8,128)(2,1)S(1)}, u32[]{:S(2)}, u32[]{:S(2)}) collective-permute-start(bf16[1024,256]{1,0:T(8,128)(2,1)S(1)} %copy-done.37), channel_id=1, source_target_pairs={{0,4},{4,0},{8,12},{12,8},{16,20},{20,16},{24,28},{28,24},{1,5},{5... | collective-permute-start | bytes 1572872 | tf_op jit(solution)/shard_map/ppermute | solution.py:23
  526.3 77.1 %collective-permute-start.47 = (bf16[1024,256]{1,0:T(8,128)(2,1)S(1)}, bf16[1024,256]{1,0:T(8,128)(2,1)S(1)}, u32[]{:S(2)}, u32[]{:S(2)}) collective-permute-start(bf16[1024,256]{1,0:T(8,128)(2,1)S(1)} %copy-done.38), channel_id=1, source_target_pairs={{0,4},{4,0},{8,12},{12,8},{16,20},{20,16},{24,28},{28,24},{1,5},{5... | collective-permute-start | bytes 1572872 | tf_op jit(solution)/shard_map/ppermute | solution.py:23
  559.8 39.3 %collective-permute-start.46 = (bf16[1344,256]{1,0:T(8,128)(2,1)S(1)}, bf16[1344,256]{1,0:T(8,128)(2,1)S(1)}, u32[]{:S(2)}, u32[]{:S(2)}) collective-permute-start(bf16[1344,256]{1,0:T(8,128)(2,1)S(1)} %add_convert_fusion), channel_id=1, source_target_pairs={{0,8},{4,12},{8,16},{12,20},{16,24},{20,28},{24,0},{28,4},{1,9},{5... | collective-permute-start | bytes 2064392 | tf_op jit(solution)/shard_map/ppermute | solution.py:150
  (102 other events, 2131.3 us)
